TPU v7x, 128 devices: a whole 4x4x4 slice. The times are simulated.
128 devices in a mesh: gx: 16 (over z, x), gy: 8 (over y, core).
Axes of the slice: x: 4, y: 4, z: 4, core: 2. Of those that a mesh axis runs over, the one named last changes fastest.
Arguments:
- velocity: bfloat16 [3, 16, 2048, 2048], P(None, None, 'gx', 'gy'), may hold values from -4 to 4
- kinetic_energy: bfloat16 [16, 2048, 2048], P(None, 'gx', 'gy'), may hold values from 0.019897461 to 0.3984375
- dissipation_rate: bfloat16 [16, 2048, 2048], P(None, 'gx', 'gy'), may hold values from 1 to 8
- adjoint_start: float32 [3, 16, 2048, 2048], P(None, None, 'gx', 'gy'), may hold values from -6 to 6
- interp_weight: bfloat16 [128, 256], replicated, may hold values from -0.375 to 0.375
- observed: float32 [3, 32768, 128], P(None, ('gx', 'gy')), may hold values from -6 to 6
- window_weight: float32 [32768], P(('gx', 'gy')), may hold values from 0.5 to 2
- window_source: int32 [32768, 1], P(('gx', 'gy')), may hold values from 0 to 127; in each aligned block of 256 rows (0 to 255, 256 to 511, ...) at most 4 rows name the same one
- window_block: int32 [32768], P(('gx', 'gy')), may hold values from 0 to 2047
- window_count: int32 [32768], P(('gx', 'gy')), may hold values from 1 to 256
Outputs:
- adjoint_end: float32 [3, 16, 2048, 2048], P(None, None, 'gx', 'gy')
Inputs may be any that keep to these rules, and one draw needn't show every extreme that they name: `window_source`: among the windows of one owner device (aligned blocks of 256 rows), at most 4 name the same source device, a bound that some block reaches.
All inputs are finite; a program needn't handle non-finite values.
Results may differ from a plain program's by a relative error of at most 0.00072.
Values may be sent and summed in bfloat16 or wider, within the bound.
A program may use at most 192 MiB of HBM per device.

v0:
```python
import jax
import jax.numpy as jnp
from jax import lax
from jax.sharding import PartitionSpec as P

SWEEPS = 2


base_viscosity = 0.05
pseudo_step = 0.4


def extended(cells, sides, width):
    for axis, dim in sides:
        count = lax.axis_size(axis)
        ends = count - 1
        head = lax.slice_in_dim(cells, 0, width, axis=dim)
        tail = lax.slice_in_dim(cells, cells.shape[dim] - width, cells.shape[dim], axis=dim)
        cells = jnp.concatenate(
            [
                lax.ppermute(tail, axis, [(i, (i + 1) % count) for i in range(ends)]),
                cells,
                lax.ppermute(head, axis, [((i + 1) % count, i) for i in range(ends)]),
            ],
            axis=dim,
        )
    return cells


def part(field, step_z, step_x, step_y):
    size_z = field.shape[1] - 2
    size_x = field.shape[2] - 2
    size_y = field.shape[3] - 2
    return field[
        :,
        1 + step_z : 1 + step_z + size_z,
        1 + step_x : 1 + step_x + size_x,
        1 + step_y : 1 + step_y + size_y,
    ]


def widen_states(state_pad):
    return jnp.pad(state_pad.astype(jnp.float32), ((0, 0), (1, 1), (0, 0), (0, 0)))


def transport(adjoint_pad, states, forcing):
    viscous = states[3:4]
    centre = adjoint_pad[:, :, 1:-1, 1:-1]
    visc_centre = part(viscous, 0, 0, 0)
    summed = forcing
    for component, shift in ((0, (0, 1, 0)), (1, (0, 0, 1)), (2, (1, 0, 0))):
        step_z, step_x, step_y = shift
        speed = states[component : component + 1]
        if step_z == 1:
            upper = jnp.pad(centre[:, 1:], ((0, 0), (0, 1), (0, 0), (0, 0)))
            lower = jnp.pad(centre[:, :-1], ((0, 0), (1, 0), (0, 0), (0, 0)))
        else:
            size_x = adjoint_pad.shape[2] - 2
            size_y = adjoint_pad.shape[3] - 2
            upper = adjoint_pad[
                :, :, 1 + step_x : 1 + step_x + size_x, 1 + step_y : 1 + step_y + size_y
            ]
            lower = adjoint_pad[
                :, :, 1 - step_x : 1 - step_x + size_x, 1 - step_y : 1 - step_y + size_y
            ]
        speed_up = part(speed, step_z, step_x, step_y)
        speed_down = part(speed, -step_z, -step_x, -step_y)
        visc_up = part(viscous, step_z, step_x, step_y)
        visc_down = part(viscous, -step_z, -step_x, -step_y)
        summed = summed + 0.5 * (speed_down * lower - speed_up * upper)
        summed = (
            summed
            + 0.5 * (visc_up + visc_centre) * (upper - centre)
            - 0.5 * (visc_centre + visc_down) * (centre - lower)
        )
    return centre + pseudo_step * summed


def local(
    velocity,
    kinetic_energy,
    dissipation_rate,
    adjoint_start,
    interp_weight,
    observed,
    window_weight,
    window_source,
    window_block,
    window_count,
):
    planes, width_x, width_y = kinetic_energy.shape
    line_cells = interp_weight.shape[1]
    peers = lax.axis_size("gx") * lax.axis_size("gy")
    windows = window_block.shape[0]
    capacity = max(2, 2 * windows // peers)
    slots = peers * capacity
    source = window_source[:, 0]
    same_source = source[:, None] == source[None, :]
    counter = jnp.arange(windows, dtype=jnp.int32)
    earlier = counter[None, :] < counter[:, None]
    slot = jnp.sum((same_source & earlier).astype(jnp.int32), axis=1)
    position = source * capacity + slot
    requests = (
        jnp.zeros((2, slots), jnp.int32)
        .at[:, position]
        .set(jnp.stack([window_block, window_count]))
    )
    arrived = lax.all_to_all(
        requests.reshape(2, peers, capacity), ("gx", "gy"), split_axis=1, concat_axis=1, tiled=True
    ).reshape(2, slots)
    wanted = arrived[0]
    wanted_count = arrived[1]
    cells = jnp.arange(line_cells, dtype=jnp.int32)
    wanted_inside = cells[None, :] < wanted_count[:, None]
    own_inside = (cells[None, :] < window_count[:, None]).astype(jnp.float32)
    own_lines = velocity.reshape(3, -1, line_cells)
    picked = own_lines[:, wanted] * wanted_inside.astype(jnp.bfloat16)[None]
    weights = interp_weight.astype(jnp.float32)
    returned = lax.all_to_all(
        picked.reshape(3, peers, capacity, line_cells),
        ("gx", "gy"),
        split_axis=1,
        concat_axis=1,
        tiled=True,
    ).reshape(3, slots, line_cells)
    window_lines = returned[:, position]
    predicted = jnp.einsum(
        "cwj,mj->cwm", window_lines, interp_weight, preferred_element_type=jnp.float32
    )
    residual = window_weight[None, :, None] * (predicted - observed)
    line_forcing = own_inside[None] * jnp.einsum(
        "cwm,mj->cwj", residual, weights, precision=lax.Precision.HIGHEST
    )
    outgoing = jnp.zeros((3, slots, line_cells), jnp.float32).at[:, position].set(line_forcing)
    incoming = lax.all_to_all(
        outgoing.reshape(3, peers, capacity, line_cells),
        ("gx", "gy"),
        split_axis=1,
        concat_axis=1,
        tiled=True,
    ).reshape(3, slots, line_cells)
    forcing = (
        jnp.zeros((3, own_lines.shape[1], line_cells), jnp.float32)
        .at[:, wanted]
        .add(incoming)
        .reshape(3, planes, width_x, width_y)
    )
    viscosity = (
        base_viscosity + kinetic_energy.astype(jnp.float32) / dissipation_rate.astype(jnp.float32)
    ).astype(jnp.bfloat16)
    states = jnp.concatenate([velocity, viscosity[None]], 0)
    state_pad = extended(states, (("gx", 2), ("gy", 3)), 1)
    widened = widen_states(state_pad)
    adjoint = adjoint_start
    for sweep in range(SWEEPS):
        adjoint_pad = extended(adjoint, (("gx", 2), ("gy", 3)), 1)
        adjoint = transport(adjoint_pad, widened, forcing)
    return adjoint


def solution(mesh):
    placed = (
        P(None, None, "gx", "gy"),
        P(None, "gx", "gy"),
        P(None, "gx", "gy"),
        P(None, None, "gx", "gy"),
        P(),
        P(None, ("gx", "gy"), None),
        P(("gx", "gy")),
        P(("gx", "gy"), None),
        P(("gx", "gy")),
        P(("gx", "gy")),
    )
    return jax.shard_map(
        local, mesh=mesh, in_specs=placed, out_specs=P(None, None, "gx", "gy"), check_vma=False
    )
```

profile of v0, /device:TPU:33, one launch (start us, length us, event | category | flops | bytes accessed | tf_op | source)
XLA Modules:
  0.0 473.2 jit_solution(17903528682953274260)
XLA Ops:
  1.8 3.9 collective-permute-start.5
  13.5 12.7 %all-to-all-start = ((s32[2,128,4]{2,0,1:T(2,128)}), s32[2,128,4]{2,0,1:T(2,128)}, u32[]{:S(2)}, u32[]{:S(2)}) async-start(s32[2,128,4]{2,0,1:T(2,128)} %copy.143), calls=%async_computation | async-start | bytes 262144 | tf_op jit(solution)/shard_map/all_to_all | solution.py:108
  26.2 3.8 copy.156
  33.0 3.1 collective-permute-start
  36.1 4.8 %collective-permute-start.1 = (bf16[4,16,1,256]{3,1,2,0:T(8,128)(2,1)}, bf16[4,16,1,256]{3,1,2,0:T(8,128)(2,1)}, u32[]{:S(2)}, u32[]{:S(2)}) collective-permute-start(bf16[4,16,1,256]{3,1,2,0:T(8,128)(2,1)} %get-tuple-element.32), channel_id=1, source_target_pairs={{8,0},{16,8},{24,16},{32,24},{40,32},{48,40},{56,48},{64,56},{72,6... | collective-permute-start | bytes 98312 | tf_op jit(solution)/shard_map/ppermute | solution.py:23
  41.1 6.6 %copy.191 = f32[3,16,128,256]{2,1,3,0:T(8,128)} copy(f32[3,16,128,256]{3,2,1,0:T(8,128)} %param.13) | data formatting | bytes 12582912 | tf_op args[3]
  47.7 10.6 %fusion.30 = (f32[3,15,128,256]{2,1,3,0:T(8,128)}, f32[3,15,128,256]{2,1,3,0:T(8,128)}) fusion(f32[3,16,128,256]{2,1,3,0:T(8,128)} %copy.191), kind=kLoop, calls=%fused_computation.89 | loop fusion | bytes 23592960 | tf_op jit(solution)/shard_map/slice | solution.py:56
  59.0 4.7 copy.144
  67.9 4.9 %gather_fusion = bf16[512,3,256]{2,1,0:T(4,128)(2,1)} fusion(bf16[3,2048,256]{2,0,1:T(4,128)(2,1)} %bitcast.60, s32[1024]{0:T(1024)S(1)} %pad_clamp_fusion.1), kind=kCustom, calls=%fused_computation | custom fusion | bytes 1574912 | tf_op jit(solution)/shard_map/gather | solution.py:117
  75.5 8.9 %all-to-all-start.1 = ((bf16[3,128,4,256]{3,2,0,1:T(4,128)(2,1)}), bf16[3,128,4,256]{3,2,0,1:T(4,128)(2,1)}, u32[]{:S(2)}, u32[]{:S(2)}) async-start(bf16[3,128,4,256]{3,2,0,1:T(4,128)(2,1)} %copy_multiply_fusion), calls=%async_computation.1 | async-start | bytes 1572864 | tf_op jit(solution)/shard_map/all_to_all | solution.py:119
  89.1 3.6 copy.157
  98.1 3.3 collective-permute-start.2
  101.4 5.5 %copy.163 = f32[3,16,1,256]{2,1,3,0:T(8,128)} copy(f32[3,16,1,256]{3,1,2,0:T(8,128)} %collective-permute-done.4) | data formatting | bytes 98304 | tf_op jit(solution)/shard_map/ppermute | solution.py:21
  106.9 5.5 %copy.168 = f32[3,16,1,256]{2,1,3,0:T(8,128)} copy(f32[3,16,1,256]{3,1,2,0:T(8,128)} %collective-permute-done.5) | data formatting | bytes 98304 | tf_op jit(solution)/shard_map/ppermute | solution.py:23
  118.5 3.7 copy.159
  122.2 3.6 copy.160
  128.3 3.3 gather_fusion.1
  136.6 26.5 %scatter_fusion = f32[3,512,256]{2,0,1:T(4,128)} fusion(f32[3,512,256]{2,0,1:T(4,128)} %broadcast_in_dim.10, s32[256]{0:T(256)S(1)} %bitcast.70, f32[256,3,256]{2,1,0:T(4,128)} %copy.150), kind=kCustom, calls=%fused_computation.3 | custom fusion | bytes 2360320 | tf_op jit(solution)/shard_map/scatter | solution.py:134
  163.1 3.1 copy.151
  166.2 10.5 %all-to-all-start.2 = ((f32[3,128,4,256]{3,2,0,1:T(4,128)}), f32[3,128,4,256]{3,2,0,1:T(4,128)}, u32[]{:S(2)}, u32[]{:S(2)}) async-start(f32[3,128,4,256]{3,2,0,1:T(4,128)} %copy.151), calls=%async_computation.2 | async-start | bytes 3145728 | tf_op jit(solution)/shard_map/all_to_all | solution.py:135
  176.8 11.0 %maximum_convert_fusion = f32[4,16,130,258]{3,1,2,0:T(8,128)} fusion(bf16[4,16,130,1]{3,1,2,0:T(8,128)(2,1)} %copy.160, bf16[4,16,1,256]{3,1,2,0:T(8,128)(2,1)} %collective-permute-done.1, bf16[1,16,128,256]{3,1,2,0:T(8,128)(2,1)} %copy-done.3, bf16[3,16,128,256]{3,1,2,0:T(8,128)(2,1)S(1)} %copy.156, bf16[4,16,1,256]{3,1,2,0:T(8,128)(2,1)} %collective-permute-done, ...), kind=kLoop, calls=%fused_computation.9 | loop fusion | flops 25758720 | bytes 12879360 | tf_op jit(solution)/shard_map/convert_element_type | solution.py:43
  187.7 26.5 %slice_bitcast_fusion.3 = (f32[16,128,256]{2,0,1:T(8,128)}, f32[16,128,256]{2,0,1:T(8,128)}, f32[16,128,256]{2,0,1:T(8,128)}, f32[16,128,256]{2,0,1:T(8,128)}, f...) fusion(f32[4,16,130,258]{3,1,2,0:T(8,128)} %maximum_convert_fusion), kind=kLoop, calls=%fused_computation.52 | loop fusion | flops 6291456 | bytes 56819712 | tf_op jit(solution)/shard_map/mul | solution.py:70
  216.8 4.1 copy.187
  220.9 3.3 copy.189
  224.3 3.4 copy.183
  227.6 3.3 copy.181
  230.9 3.3 copy.179
  234.3 3.3 copy.178
  237.6 3.4 copy.174
  241.0 3.4 copy.172
  244.4 3.3 copy.185
  247.7 3.3 copy.170
  251.0 3.5 copy.165
  260.0 3.8 copy.153
  263.9 4.0 broadcast_in_dim.8
  267.8 59.7 %scatter_fusion.1 = f32[3,2048,256]{2,0,1:T(4,128)} fusion(f32[3,2048,256]{2,0,1:T(4,128)} %broadcast_in_dim.8, s32[512]{0:T(512)S(1)} %bitcast.67, f32[512,3,256]{2,1,0:T(4,128)} %copy.153), kind=kCustom, calls=%fused_computation.4 | custom fusion | flops 393216 | bytes 4720640 | tf_op jit(solution)/shard_map/scatter-add | solution.py:145
  327.5 7.2 %copy.169 = f32[3,16,128,256]{2,1,3,0:T(8,128)} copy(f32[3,16,128,256]{3,0,2,1:T(4,128)} %bitcast.57) | data formatting | bytes 12582912 | tf_op jit(solution)/shard_map/reshape | solution.py:146
  334.8 39.1 %multiply_add_fusion.1 = f32[3,16,128,256]{2,1,3,0:T(8,128)} fusion(f32[3,16,128,256]{2,1,3,0:T(8,128)} %copy.191, f32[3,15,128,256]{2,1,3,0:T(8,128)} %get-tuple-element.28, f32[3,15,128,256]{2,1,3,0:T(8,128)} %get-tuple-element.27, f32[3,16,130,1]{2,1,3,0:T(8,128)} %collective-permute-done.7, f32[3,16,1,256]{2,1,3,0:T(8,128)} %copy.168, ...), kind=kLoop, calls=%fused_computation.27 | loop fusion | flops 67633152 | bytes 55984896 | tf_op jit(solution)/shard_map/add | solution.py:76
  373.9 11.0 %fusion.27 = (f32[3,16,1,256]{2,1,3,0:T(8,128)}, f32[3,16,1,256]{2,1,3,0:T(8,128)}) fusion(f32[3,16,128,256]{2,1,3,0:T(8,128)} %multiply_add_fusion.1), kind=kLoop, calls=%fused_computation.86 | loop fusion | bytes 196608 | tf_op jit(solution)/shard_map/slice | solution.py:18
  384.9 5.1 %copy.192 = f32[3,16,1,256]{3,1,2,0:T(8,128)S(1)} copy(f32[3,16,1,256]{2,1,3,0:T(8,128)} %get-tuple-element.21) | data formatting | bytes 98304 | tf_op jit(solution)/shard_map/slice | solution.py:18
  390.0 7.4 %collective-permute-start.8 = (f32[3,16,1,256]{3,1,2,0:T(8,128)S(1)}, f32[3,16,1,256]{3,1,2,0:T(8,128)S(1)}, u32[]{:S(2)}, u32[]{:S(2)}) collective-permute-start(f32[3,16,1,256]{3,1,2,0:T(8,128)S(1)} %copy.192), channel_id=1, source_target_pairs={{0,8},{8,16},{16,24},{24,32},{32,40},{40,48},{48,56},{56,64},{64,7... | collective-permute-start | bytes 147464 | tf_op jit(solution)/shard_map/ppermute | solution.py:21
  397.4 5.1 %copy.194 = f32[3,16,1,256]{3,1,2,0:T(8,128)S(1)} copy(f32[3,16,1,256]{2,1,3,0:T(8,128)} %get-tuple-element.22) | data formatting | bytes 98304 | tf_op jit(solution)/shard_map/slice | solution.py:17
  404.5 4.8 %copy.193 = f32[3,16,1,256]{2,1,3,0:T(8,128)} copy(f32[3,16,1,256]{3,1,2,0:T(8,128)S(1)} %collective-permute-done.8) | data formatting | bytes 98304 | tf_op jit(solution)/shard_map/ppermute | solution.py:21
  409.3 4.9 %copy.195 = f32[3,16,1,256]{2,1,3,0:T(8,128)} copy(f32[3,16,1,256]{3,1,2,0:T(8,128)S(1)} %collective-permute-done.9) | data formatting | bytes 98304 | tf_op jit(solution)/shard_map/ppermute | solution.py:23
  415.2 6.9 %collective-permute-start.10 = (f32[3,16,130,1]{2,1,3,0:T(8,128)S(1)}, f32[3,16,130,1]{2,1,3,0:T(8,128)S(1)}, u32[]{:S(2)}, u32[]{:S(2)}) collective-permute-start(f32[3,16,130,1]{2,1,3,0:T(8,128)S(1)} %get-tuple-element.5), channel_id=1, source_target_pairs={{0,1},{1,2},{2,3},{3,4},{4,5},{5,6},{6,7},{8,9},{9,10},{10,11},{11... | collective-permute-start | bytes 74888 | tf_op jit(solution)/shard_map/ppermute | solution.py:21
  424.1 5.8 %fusion.28 = (f32[3,15,128,256]{2,1,3,0:T(8,128)}, f32[3,15,128,256]{2,1,3,0:T(8,128)}) fusion(f32[3,16,128,256]{2,1,3,0:T(8,128)S(1)} %bitcast.56), kind=kLoop, calls=%fused_computation.87 | loop fusion | bytes 23592960 | tf_op jit(solution)/shard_map/slice | solution.py:56
  430.0 36.1 %multiply_add_fusion = f32[3,16,128,256]{2,1,3,0:T(8,128)} fusion(f32[3,16,128,256]{2,1,3,0:T(8,128)} %multiply_add_fusion.1, f32[3,15,128,256]{2,1,3,0:T(8,128)} %get-tuple-element.24, f32[3,15,128,256]{2,1,3,0:T(8,128)} %get-tuple-element.23, f32[3,16,130,1]{2,1,3,0:T(8,128)S(1)} %collective-permute-done.11, f32[3,16,1,256]{2,1,3,0:T(8,128)} %copy.195, ...), kind=kLoop, calls=%fused_computation.26 | loop fusion | flops 67633152 | bytes 55984896 | tf_op jit(solution)/shard_map/add | solution.py:76
  466.1 6.6 %copy.199 = f32[3,16,128,256]{3,2,1,0:T(8,128)} copy(f32[3,16,128,256]{2,1,3,0:T(8,128)} %multiply_add_fusion) | data formatting | bytes 12582912 | tf_op jit(solution)/shard_map/add | solution.py:76
  (82 shorter events, 56.7 us)
Async XLA Ops:
  0.0 131.6 %copy-start = (bf16[128,256]{1,0:T(8,128)(2,1)S(1)}, bf16[128,256]{1,0:T(8,128)(2,1)}, u32[]{:S(2)}) copy-start(bf16[128,256]{1,0:T(8,128)(2,1)} %param.14) | copy-start | bytes 196612
  1.8 105.0 %collective-permute-start.5 = (f32[3,16,1,256]{3,1,2,0:T(8,128)}, f32[3,16,1,256]{3,1,2,0:T(8,128)}, u32[]{:S(2)}, u32[]{:S(2)}) collective-permute-start(f32[3,16,1,256]{3,1,2,0:T(8,128)} %copy.202), channel_id=1, source_target_pairs={{8,0},{16,8},{24,16},{32,24},{40,32},{48,40},{56,48},{64,56},{72,6... | collective-permute-start | bytes 147464 | tf_op jit(solution)/shard_map/ppermute | solution.py:23
  6.4 95.0 %collective-permute-start.4 = (f32[3,16,1,256]{3,1,2,0:T(8,128)}, f32[3,16,1,256]{3,1,2,0:T(8,128)}, u32[]{:S(2)}, u32[]{:S(2)}) collective-permute-start(f32[3,16,1,256]{3,1,2,0:T(8,128)} %copy.201), channel_id=1, source_target_pairs={{0,8},{8,16},{16,24},{24,32},{32,40},{40,48},{48,56},{56,64},{64,7... | collective-permute-start | bytes 147464 | tf_op jit(solution)/shard_map/ppermute | solution.py:21
  9.9 48.4 %copy-start.9 = (s32[256,1]{0,1:T(1,128)}, s32[256,1]{0,1:T(1,128)S(1)}, u32[]{:S(2)}) copy-start(s32[256,1]{0,1:T(1,128)S(1)} %compare_select_fusion.1) | copy-start | bytes 3076
  13.5 50.1 %all-to-all-start = ((s32[2,128,4]{2,0,1:T(2,128)}), s32[2,128,4]{2,0,1:T(2,128)}, u32[]{:S(2)}, u32[]{:S(2)}) async-start(s32[2,128,4]{2,0,1:T(2,128)} %copy.143), calls=%async_computation | async-start | bytes 262144 | tf_op jit(solution)/shard_map/all_to_all | solution.py:108
  26.2 3.9 copy-start.5
  26.2 3.9 copy-start.6
  26.2 14.7 %copy-start.11 = (s32[256]{0:T(256)S(1)}, s32[256]{0:T(256)}, u32[]{:S(2)}) copy-start(s32[256]{0:T(256)} %param.19) | copy-start | bytes 3076
  31.4 1.0 copy-start.3
  33.0 51.3 %collective-permute-start = (bf16[4,16,1,256]{3,1,2,0:T(8,128)(2,1)}, bf16[4,16,1,256]{3,1,2,0:T(8,128)(2,1)}, u32[]{:S(2)}, u32[]{:S(2)}) collective-permute-start(bf16[4,16,1,256]{3,1,2,0:T(8,128)(2,1)} %get-tuple-element.31), channel_id=1, source_target_pairs={{0,8},{8,16},{16,24},{24,32},{32,40},{40,48},{48,56},{56,64},{64,7... | collective-permute-start | bytes 98312 | tf_op jit(solution)/shard_map/ppermute | solution.py:21
  36.1 48.2 %collective-permute-start.1 = (bf16[4,16,1,256]{3,1,2,0:T(8,128)(2,1)}, bf16[4,16,1,256]{3,1,2,0:T(8,128)(2,1)}, u32[]{:S(2)}, u32[]{:S(2)}) collective-permute-start(bf16[4,16,1,256]{3,1,2,0:T(8,128)(2,1)} %get-tuple-element.32), channel_id=1, source_target_pairs={{8,0},{16,8},{24,16},{32,24},{40,32},{48,40},{56,48},{64,56},{72,6... | collective-permute-start | bytes 98312 | tf_op jit(solution)/shard_map/ppermute | solution.py:23
  47.7 11.2 %copy-start.4 = (bf16[3,16,128,256]{3,2,1,0:T(8,128)(2,1)S(1)}, bf16[3,16,128,256]{3,2,1,0:T(8,128)(2,1)}, u32[]{:S(2)}) copy-start(bf16[3,16,128,256]{3,2,1,0:T(8,128)(2,1)} %param.10) | copy-start | bytes 9437188
  66.4 0.6 copy-start.7
  75.5 50.3 %all-to-all-start.1 = ((bf16[3,128,4,256]{3,2,0,1:T(4,128)(2,1)}), bf16[3,128,4,256]{3,2,0,1:T(4,128)(2,1)}, u32[]{:S(2)}, u32[]{:S(2)}) async-start(bf16[3,128,4,256]{3,2,0,1:T(4,128)(2,1)} %copy_multiply_fusion), calls=%async_computation.1 | async-start | bytes 1572864 | tf_op jit(solution)/shard_map/all_to_all | solution.py:119
  95.8 26.4 %collective-permute-start.3 = (bf16[4,16,130,1]{2,1,3,0:T(8,128)(2,1)S(1)}, bf16[4,16,130,1]{2,1,3,0:T(8,128)(2,1)}, u32[]{:S(2)}, u32[]{:S(2)}) collective-permute-start(bf16[4,16,130,1]{2,1,3,0:T(8,128)(2,1)S(1)} %copy.158), channel_id=1, source_target_pairs={{1,0},{2,1},{3,2},{4,3},{5,4},{6,5},{7,6},{9,8},{10,9},{11,10},{12... | collective-permute-start | bytes 49928 | tf_op jit(solution)/shard_map/ppermute | solution.py:23
  98.1 20.4 %collective-permute-start.2 = (bf16[4,16,130,1]{2,1,3,0:T(8,128)(2,1)}, bf16[4,16,130,1]{2,1,3,0:T(8,128)(2,1)}, u32[]{:S(2)}, u32[]{:S(2)}) collective-permute-start(bf16[4,16,130,1]{2,1,3,0:T(8,128)(2,1)} %copy.157), channel_id=1, source_target_pairs={{0,1},{1,2},{2,3},{3,4},{4,5},{5,6},{6,7},{8,9},{9,10},{10,11},{11... | collective-permute-start | bytes 49928 | tf_op jit(solution)/shard_map/ppermute | solution.py:21
  114.0 220.8 %collective-permute-start.6 = (f32[3,16,130,1]{2,1,3,0:T(8,128)}, f32[3,16,130,1]{2,1,3,0:T(8,128)S(1)}, u32[]{:S(2)}, u32[]{:S(2)}) collective-permute-start(f32[3,16,130,1]{2,1,3,0:T(8,128)} %get-tuple-element.7), channel_id=1, source_target_pairs={{0,1},{1,2},{2,3},{3,4},{4,5},{5,6},{6,7},{8,9},{9,10},{10,11},{11... | collective-permute-start | bytes 74888 | tf_op jit(solution)/shard_map/ppermute | solution.py:21
  116.1 218.6 %collective-permute-start.7 = (f32[3,16,130,1]{2,1,3,0:T(8,128)}, f32[3,16,130,1]{2,1,3,0:T(8,128)}, u32[]{:S(2)}, u32[]{:S(2)}) collective-permute-start(f32[3,16,130,1]{2,1,3,0:T(8,128)} %get-tuple-element.8), channel_id=1, source_target_pairs={{1,0},{2,1},{3,2},{4,3},{5,4},{6,5},{7,6},{9,8},{10,9},{11,10},{12... | collective-permute-start | bytes 74888 | tf_op jit(solution)/shard_map/ppermute | solution.py:23
  122.1 14.5 %copy-start.10 = (s32[256,1]{0,1:T(1,128)S(1)}, s32[256,1]{0,1:T(1,128)}, u32[]{:S(2)}) copy-start(s32[256,1]{0,1:T(1,128)} %copy-done.9) | copy-start | bytes 3076
  166.2 88.2 %all-to-all-start.2 = ((f32[3,128,4,256]{3,2,0,1:T(4,128)}), f32[3,128,4,256]{3,2,0,1:T(4,128)}, u32[]{:S(2)}, u32[]{:S(2)}) async-start(f32[3,128,4,256]{3,2,0,1:T(4,128)} %copy.151), calls=%async_computation.2 | async-start | bytes 3145728 | tf_op jit(solution)/shard_map/all_to_all | solution.py:135
  216.8 117.9 %copy-start.2 = (f32[16,128,256]{1,0,2:T(8,128)}, f32[16,128,256]{1,0,2:T(8,128)S(1)}, u32[]{:S(2)}) copy-start(f32[16,128,256]{1,0,2:T(8,128)S(1)} %copy.161) | copy-start | bytes 6291460
  260.0 7.8 %copy-start.8 = (s32[512,1]{0,1:T(1,128)S(1)}, s32[512,1]{0,1:T(1,128)}, u32[]{:S(2)}) copy-start(s32[512,1]{0,1:T(1,128)} %copy-done.7) | copy-start | bytes 6148
  390.0 14.5 %collective-permute-start.8 = (f32[3,16,1,256]{3,1,2,0:T(8,128)S(1)}, f32[3,16,1,256]{3,1,2,0:T(8,128)S(1)}, u32[]{:S(2)}, u32[]{:S(2)}) collective-permute-start(f32[3,16,1,256]{3,1,2,0:T(8,128)S(1)} %copy.192), channel_id=1, source_target_pairs={{0,8},{8,16},{16,24},{24,32},{32,40},{40,48},{48,56},{56,64},{64,7... | collective-permute-start | bytes 147464 | tf_op jit(solution)/shard_map/ppermute | solution.py:21
  402.6 6.7 %collective-permute-start.9 = (f32[3,16,1,256]{3,1,2,0:T(8,128)S(1)}, f32[3,16,1,256]{3,1,2,0:T(8,128)S(1)}, u32[]{:S(2)}, u32[]{:S(2)}) collective-permute-start(f32[3,16,1,256]{3,1,2,0:T(8,128)S(1)} %copy.194), channel_id=1, source_target_pairs={{8,0},{16,8},{24,16},{32,24},{40,32},{48,40},{56,48},{64,56},{72,6... | collective-permute-start | bytes 147464 | tf_op jit(solution)/shard_map/ppermute | solution.py:23
  409.3 14.8 %slice-start = ((s8[6291456]{0:T(1024)(128)(4,1)}), s8[2097152]{0:T(1024)(128)(4,1)S(1)}, s32[]{:S(2)}) async-start(s8[6291456]{0:T(1024)(128)(4,1)} %bitcast.55), calls=%async_computation.3 | async-start | bytes 4194304
  414.2 10.0 %slice-start.1 = ((s8[6291456]{0:T(1024)(128)(4,1)}), s8[4194304]{0:T(1024)(128)(4,1)S(1)}, s32[]{:S(2)}) async-start(s8[6291456]{0:T(1024)(128)(4,1)} %bitcast.55), calls=%async_computation.4 | async-start | bytes 8388608
  415.2 14.8 %collective-permute-start.10 = (f32[3,16,130,1]{2,1,3,0:T(8,128)S(1)}, f32[3,16,130,1]{2,1,3,0:T(8,128)S(1)}, u32[]{:S(2)}, u32[]{:S(2)}) collective-permute-start(f32[3,16,130,1]{2,1,3,0:T(8,128)S(1)} %get-tuple-element.5), channel_id=1, source_target_pairs={{0,1},{1,2},{2,3},{3,4},{4,5},{5,6},{6,7},{8,9},{9,10},{10,11},{11... | collective-permute-start | bytes 74888 | tf_op jit(solution)/shard_map/ppermute | solution.py:21
  422.2 7.8 %collective-permute-start.11 = (f32[3,16,130,1]{2,1,3,0:T(8,128)S(1)}, f32[3,16,130,1]{2,1,3,0:T(8,128)S(1)}, u32[]{:S(2)}, u32[]{:S(2)}) collective-permute-start(f32[3,16,130,1]{2,1,3,0:T(8,128)S(1)} %get-tuple-element.6), channel_id=1, source_target_pairs={{1,0},{2,1},{3,2},{4,3},{5,4},{6,5},{7,6},{9,8},{10,9},{11,10},{12... | collective-permute-start | bytes 74888 | tf_op jit(solution)/shard_map/ppermute | solution.py:23
  430.0 42.7 %copy-start.1 = (bf16[128,256]{1,0:T(8,128)(2,1)S(1)}, bf16[128,256]{1,0:T(8,128)(2,1)}, u32[]{:S(2)}) copy-start(bf16[128,256]{1,0:T(8,128)(2,1)} %param.14) | copy-start | bytes 196612
where the time goes:
time: 482 us; the launch traced here: 473 us
  local copies, waits for them, and re-layouts  211 us (44%)
  other arithmetic  185 us (38%)
  starting transfers between devices  74 us (15%)
    add x2, other arithmetic, transport(): return centre + pseudo_step * summed  75.2 us
    scatter-add x1, other arithmetic, local(): forcing = jnp.zeros((3, own_lines.shape[1], line_cells), jnp.float32).at[...  59.7 us
    mul x1, other arithmetic, transport(): summed = summed + 0.5 * (speed_down * lower - speed_up * upper)  26.5 us
    scatter x1, local copies, waits for them, and re-layouts, local(): jnp.zeros((3, slots, line_cells), jnp.float32).at[:, position]  26.5 us
    ppermute x6, starting transfers between devices, extended(): lax.ppermute(tail, axis, [(i, (i + 1) % count) for i in range(ends)])  24.8 us
    slice x5, local copies, waits for them, and re-layouts, extended(): lax.slice_in_dim(cells, cells.shape[dim] - width, cells.shape[dim], axis=...  23.9 us
    mul x6, local copies, waits for them, and re-layouts, transport(): summed = summed + 0.5 * (speed_down * lower - speed_up * upper)  19.4 us
    unnamed x33, local copies, waits for them, and re-layouts  18 us
  transfers between devices with their start and end apart: 15, of which 0 were waited for; matrix products, arithmetic and copies ran while one was open for 61% of the time, Pallas kernels for 0%

commit v1 on v0

v1 whole, which is shorter than its diff:
```python
import functools

import jax
import jax.numpy as jnp
from jax import lax
from jax.experimental import pallas as pl
from jax.experimental.pallas import tpu as pltpu
from jax.sharding import PartitionSpec as P

MESH = pl.DeviceIdType.MESH
SWEEPS = 2
CAP = 4
LANES = 128
SUB = 8

base_viscosity = 0.05
pseudo_step = 0.4
half_step = 0.5 * pseudo_step

META = 385
PAD = 8


def lane_iota(rows=SUB):
    return lax.broadcasted_iota(jnp.int32, (rows, LANES), 1)


def split(x, pieces):
    out = []
    for _ in range(pieces):
        piece = x.astype(jnp.bfloat16)
        out.append(piece)
        x = x - piece.astype(jnp.float32)
    return out


def put_row(ref, side, number, row, lanes=slice(None)):
    base = pl.multiple_of(number // SUB * SUB, SUB)
    old = ref[side, pl.ds(base, SUB), lanes]
    here = lax.broadcasted_iota(jnp.int32, old.shape, 0) == number - base
    ref[side, pl.ds(base, SUB), lanes] = jnp.where(here, jnp.broadcast_to(row, old.shape), old)


def fill_slots(meta_ref, obs_ref, slots_ref, peers):
    windows = meta_ref.shape[1]
    meta = meta_ref[...]
    source_row = meta[0:1]
    columns = jnp.concatenate(
        [meta, jnp.zeros((LANES - meta.shape[0], windows), jnp.float32)], axis=0
    ).T
    source_col = columns[:, 0:1]
    first = lax.broadcasted_iota(jnp.int32, (windows, windows), 0)
    second = lax.broadcasted_iota(jnp.int32, (windows, windows), 1)
    same = (source_col == source_row) & (first < second)
    place = jnp.sum(same.astype(jnp.float32), axis=0, keepdims=True)
    slot = (source_row * CAP + place).astype(jnp.int32)
    slots = peers * CAP
    chosen = (lax.broadcasted_iota(jnp.int32, (slots, windows), 0) == slot).astype(jnp.bfloat16)
    for part in range(4):
        values = columns if part == 3 else obs_ref[part]
        total = jnp.zeros((slots, LANES), jnp.float32)
        for piece in reversed(split(values, 3)):
            total = total + jnp.dot(chosen, piece, preferred_element_type=jnp.float32)
        slots_ref[:, part * LANES : (part + 1) * LANES] = total


def prep_kernel(meta_ref, obs_ref, ux_ref, uy_ref, ke_ref, dr_ref, a_ref, slots_ref, visc_ref, xe_ref, ye_ref):
    z = pl.program_id(0)
    planes = pl.num_programs(0)
    rows, cols = ke_ref.shape[1:]

    @pl.when(z == 0)
    def _():
        fill_slots(meta_ref, obs_ref, slots_ref, slots_ref.shape[0] // CAP)

    visc = (
        base_viscosity + ke_ref[0].astype(jnp.float32) / dr_ref[0].astype(jnp.float32)
    ).astype(jnp.bfloat16)
    visc_ref[0] = visc
    fields = [a_ref[c, 0] for c in range(3)]
    @pl.when(z == 0)
    def _():
        xe_ref[...] = jnp.zeros_like(xe_ref)
        ye_ref[...] = jnp.zeros_like(ye_ref)

    for side, at in ((0, 0), (1, rows - 1)):
        for c in range(3):
            put_row(xe_ref, side, c * planes + z, fields[c][at : at + 1])
        put_row(xe_ref, side, 3 * planes + z, ux_ref[0, 0].astype(jnp.float32)[at : at + 1])
        put_row(xe_ref, side, 4 * planes + z, visc.astype(jnp.float32)[at : at + 1])
    fields = fields + [uy_ref[0, 0].astype(jnp.float32), visc.astype(jnp.float32)]
    lanes = lane_iota(rows)
    for side in range(2):
        total = ye_ref[side]
        for k, field in enumerate(fields):
            part = field[:, :LANES] if side == 0 else field[:, cols - LANES :]
            lane = k * planes + z
            moved = pltpu.roll(part, lane if side == 0 else lane + 1, axis=1)
            total = jnp.where(lanes == lane, moved, total)
        ye_ref[side] = total


def prep(meta, observed, velocity, kinetic_energy, dissipation_rate, adjoint, peers):
    planes, rows, cols = kinetic_energy.shape
    windows = meta.shape[1]
    plane = pl.BlockSpec((1, rows, cols), lambda z: (z, 0, 0))
    return pl.pallas_call(
        prep_kernel,
        name="prep",
        grid=(planes,),
        in_specs=[
            pl.BlockSpec((8, windows), lambda z: (0, 0)),
            pl.BlockSpec((3, windows, LANES), lambda z: (0, 0, 0)),
            pl.BlockSpec((1, 1, rows, cols), lambda z: (0, z, 0, 0)),
            pl.BlockSpec((1, 1, rows, cols), lambda z: (1, z, 0, 0)),
            plane,
            plane,
            pl.BlockSpec((3, 1, rows, cols), lambda z: (0, z, 0, 0)),
        ],
        out_specs=[
            pl.BlockSpec((peers * CAP, 4 * LANES), lambda z: (0, 0)),
            plane,
            pl.BlockSpec((2, 5 * planes, cols), lambda z: (0, 0, 0)),
            pl.BlockSpec((2, rows, LANES), lambda z: (0, 0, 0)),
        ],
        out_shape=[
            jax.ShapeDtypeStruct((peers * CAP, 4 * LANES), jnp.float32),
            jax.ShapeDtypeStruct((planes, rows, cols), jnp.bfloat16),
            jax.ShapeDtypeStruct((2, 5 * planes, cols), jnp.float32),
            jax.ShapeDtypeStruct((2, rows, LANES), jnp.float32),
        ],
        compiler_params=pltpu.CompilerParams(vmem_limit_bytes=32 << 20),
    )(meta, observed, velocity, velocity, kinetic_energy, dissipation_rate, adjoint)


def exchange_kernel(n_gx, n_gy, with_slots, *refs):
    if with_slots:
        s_ref, xe_ref, ye_ref, r_ref, xh_ref, yh_ref, send, recv, all_send, all_recv, local = refs
    else:
        xe_ref, ye_ref, xh_ref, yh_ref, send, recv = refs
    gx, gy = lax.axis_index("gx"), lax.axis_index("gy")
    me = gx * n_gy + gy
    peers = n_gx * n_gy

    def device(step):
        peer = lax.rem(me + step, peers)
        return peer, (peer // n_gy, lax.rem(peer, n_gy))

    lower_x = (lax.rem(gx + n_gx - 1, n_gx), gy)
    upper_x = (lax.rem(gx + 1, n_gx), gy)
    lower_y = (gx, lax.rem(gy + n_gy - 1, n_gy))
    upper_y = (gx, lax.rem(gy + 1, n_gy))
    sides = (
        (xe_ref.at[1], xh_ref.at[0], upper_x),
        (xe_ref.at[0], xh_ref.at[1], lower_x),
        (ye_ref.at[1], yh_ref.at[0], upper_y),
        (ye_ref.at[0], yh_ref.at[1], lower_y),
    )
    barrier = pltpu.get_barrier_semaphore()
    if with_slots:

        @pl.loop(1, peers)
        def _(step):
            pl.semaphore_signal(barrier, inc=1, device_id=device(step)[1], device_id_type=MESH)

        pl.semaphore_wait(barrier, peers - 1)
    else:
        for _, _, where in sides:
            pl.semaphore_signal(barrier, inc=1, device_id=where, device_id_type=MESH)
        pl.semaphore_wait(barrier, 4)
    copies = []
    for k, (source, target, where) in enumerate(sides):
        copy = pltpu.make_async_remote_copy(
            source, target, send.at[k], recv.at[k], device_id=where, device_id_type=MESH
        )
        copy.start()
        copies.append(copy)
    if with_slots:
        own = pltpu.make_async_copy(s_ref.at[me], r_ref.at[me], local)
        own.start()

        @pl.loop(1, peers)
        def _(step):
            peer, where = device(step)
            pltpu.make_async_remote_copy(
                s_ref.at[peer], r_ref.at[me], all_send, all_recv, device_id=where, device_id_type=MESH
            ).start()

        own.wait()
        rest = pl.ds(0, peers - 1)
        pltpu.make_async_copy(s_ref.at[rest], s_ref.at[rest], all_send).wait()
        pltpu.make_async_copy(r_ref.at[rest], r_ref.at[rest], all_recv).wait()
    for copy in copies:
        copy.wait()


def exchange(xe, ye, slots, n_gx, n_gy, collective_id):
    arrays = ([slots] if slots is not None else []) + [xe, ye]
    dma = pltpu.SemaphoreType.DMA
    scratch = [dma((4,)), dma((4,))] + ([dma, dma, dma] if slots is not None else [])
    any_space = pl.BlockSpec(memory_space=pl.ANY)
    return pl.pallas_call(
        functools.partial(exchange_kernel, n_gx, n_gy, slots is not None),
        name="exchange_slots" if slots is not None else "exchange_edges",
        in_specs=[any_space] * len(arrays),
        out_specs=[any_space] * len(arrays),
        out_shape=[jax.ShapeDtypeStruct(a.shape, a.dtype) for a in arrays],
        scratch_shapes=scratch,
        compiler_params=pltpu.CompilerParams(collective_id=collective_id, has_side_effects=True),
    )(*arrays)


def line_forcing(recv_ref, vel_ref, weight_ref, high_ref, low_ref):
    slots = recv_ref.shape[0]
    planes, rows, cols = vel_ref.shape[1:]
    weights = weight_ref[...]
    block = recv_ref[:, META : META + 1].astype(jnp.int32)
    count = recv_ref[:, META + 1 : META + 2].astype(jnp.int32)
    scale = recv_ref[:, META + 2 : META + 3]
    inside = lax.broadcasted_iota(jnp.int32, (slots, cols), 1) < count
    group = 4
    lines = [jnp.zeros((slots, cols), jnp.float32) for _ in range(3)]
    for q in range(planes // group):
        number = lax.broadcasted_iota(jnp.int32, (slots, group * rows), 1) + q * group * rows
        chosen = (number == block).astype(jnp.bfloat16)
        for c in range(3):
            some = vel_ref[c, q * group : (q + 1) * group].reshape(group * rows, cols)
            lines[c] = lines[c] + jnp.dot(chosen, some, preferred_element_type=jnp.float32)
    for c in range(3):
        masked = jnp.where(inside, lines[c], 0.0).astype(jnp.bfloat16)
        predicted = lax.dot_general(
            masked, weights, (((1,), (1,)), ((), ())), preferred_element_type=jnp.float32
        )
        residual = scale * (predicted - recv_ref[:, c * LANES : (c + 1) * LANES])
        high, low = split(residual, 2)
        placed = jnp.dot(low, weights, preferred_element_type=jnp.float32)
        placed = placed + jnp.dot(high, weights, preferred_element_type=jnp.float32)
        high, low = split(jnp.where(inside, pseudo_step * placed, 0.0), 2)
        high_ref[:, c * cols : (c + 1) * cols] = high
        low_ref[:, c * cols : (c + 1) * cols] = low


def place_lines(recv_ref, high_ref, low_ref, forcing_ref):
    slots = recv_ref.shape[0]
    lines = forcing_ref.shape[0]
    block = recv_ref[:, 3 * LANES :].T[1:2].astype(jnp.int32)
    step = 512
    for q in range(lines // step):
        number = lax.broadcasted_iota(jnp.int32, (step, slots), 0) + q * step
        chosen = (number == block).astype(jnp.bfloat16)
        for c in range(3):
            at = pl.ds(c * 256, 256)
            total = jnp.dot(chosen, low_ref[:, at], preferred_element_type=jnp.float32)
            total = total + jnp.dot(chosen, high_ref[:, at], preferred_element_type=jnp.float32)
            forcing_ref[q * step : (q + 1) * step, at] = total


def halves(x):
    return x[:, :LANES], x[:, LANES:]


def up_down(pair, below, above, first, last):
    left, right = pair
    left_up, right_up = pltpu.roll(left, LANES - 1, axis=1), pltpu.roll(right, LANES - 1, axis=1)
    left_down, right_down = pltpu.roll(left, 1, axis=1), pltpu.roll(right, 1, axis=1)
    up = (jnp.where(last, right_up, left_up), jnp.where(last, above, right_up))
    down = (jnp.where(first, below, left_down), jnp.where(first, left_down, right_down))
    return up, down


def sweep_plane(z, planes, rows, adj, ux, uy, uz, vv, yh, forcing, out, xe, ye):
    lanes = lane_iota()
    first, last = lanes == 0, lanes == LANES - 1
    here = z + 1

    def pair(ref, *index):
        return ref[(*index, slice(0, LANES))], ref[(*index, slice(LANES, 2 * LANES))]

    for r in range(rows // SUB):
        at = slice(r * SUB, (r + 1) * SUB)
        mid = slice(PAD + r * SUB, PAD + (r + 1) * SUB)
        plus = slice(PAD + r * SUB + 1, PAD + (r + 1) * SUB + 1)
        minus = slice(PAD + r * SUB - 1, PAD + (r + 1) * SUB - 1)
        edge_low, edge_high = yh[0, at, :], yh[1, at, :]

        def outside(k):
            lane = k * planes + z
            return (
                pltpu.roll(edge_low, LANES - lane, axis=1),
                pltpu.roll(edge_high, LANES - 1 - lane, axis=1),
            )

        v = pair(vv, here, mid)
        v_xp, v_xm = pair(vv, here, plus), pair(vv, here, minus)
        v_zp, v_zm = pair(vv, here + 1, mid), pair(vv, here - 1, mid)
        v_yp, v_ym = up_down(v, *outside(4), first, last)
        u_xp, u_xm = pair(ux, here, plus), pair(ux, here, minus)
        u_yp, u_ym = up_down(pair(uy, here, at), *outside(3), first, last)
        u_zp, u_zm = pair(uz, here + 1, at), pair(uz, here - 1, at)
        coef = []
        for h in range(2):
            n = [v[h] + w[h] for w in (v_xp, v_xm, v_yp, v_ym, v_zp, v_zm)]
            centre = 1.0 - ((n[0] + n[1]) + (n[2] + n[3]) + (n[4] + n[5]))
            coef.append(
                (
                    centre,
                    n[0] - u_xp[h],
                    n[1] + u_xm[h],
                    n[2] - u_yp[h],
                    n[3] + u_ym[h],
                    n[4] - u_zp[h],
                    n[5] + u_zm[h],
                )
            )
        if ye is not None:
            packed = [ye[0, at, :], ye[1, at, :]]
        for c in range(3):
            a = pair(adj, c, here, mid)
            a_xp, a_xm = pair(adj, c, here, plus), pair(adj, c, here, minus)
            a_zp, a_zm = pair(adj, c, here + 1, mid), pair(adj, c, here - 1, mid)
            a_yp, a_ym = up_down(a, *outside(c), first, last)
            new = []
            for h in range(2):
                k = coef[h]
                value = k[0] * a[h] + (k[1] * a_xp[h] + k[2] * a_xm[h])
                value = value + (k[3] * a_yp[h] + k[4] * a_ym[h])
                value = value + (k[5] * a_zp[h] + k[6] * a_zm[h])
                lane = c * 2 * LANES + h * LANES
                value = value + forcing(r, lane)
                out[c, z, at, h * LANES : (h + 1) * LANES] = value
                new.append(value)
            if ye is not None:
                lane = c * planes + z
                packed[0] = jnp.where(lanes == lane, pltpu.roll(new[0], lane, axis=1), packed[0])
                packed[1] = jnp.where(lanes == lane, pltpu.roll(new[1], lane + 1, axis=1), packed[1])
                for h in range(2):
                    half = slice(h * LANES, (h + 1) * LANES)
                    if r == 0:
                        put_row(xe, 0, lane, new[h][0:1], half)
                    if r == rows // SUB - 1:
                        put_row(xe, 1, lane, new[h][SUB - 1 : SUB], half)
        if ye is not None:
            ye[0, at, :], ye[1, at, :] = packed


def sweep_kernel(n_gx, n_gy, leading, *refs):
    if leading:
        (recv_in, weight_ref, vel_in, visc_in, adj_in, xh_ref, yh_ref,
         out_hbm, f_hbm, xe_ref, ye_ref,
         vel, visc, adj, ux, uy, uz, vv, yh, out, frc, high, low, load, save, fsave) = refs
    else:
        (f_hbm, vel_in, visc_in, adj_in, xh_ref, yh_ref, xa_ref, ya_ref,
         out_hbm,
         vel, visc, adj, ux, uy, uz, vv, yh, out, frc, load, save, fload) = refs
    planes, rows, cols = visc.shape
    gx, gy = lax.axis_index("gx"), lax.axis_index("gy")
    copies = []
    for z in range(planes):
        copies.append(
            [
                pltpu.make_async_copy(vel_in.at[:, z], vel.at[:, z], load.at[0, z]),
                pltpu.make_async_copy(visc_in.at[z], visc.at[z], load.at[1, z]),
                pltpu.make_async_copy(adj_in.at[:, z], adj.at[:, z + 1, pl.ds(PAD, rows), :], load.at[2, z]),
            ]
        )
    if leading:
        for which in range(3):
            for z in range(planes):
                copies[z][which].start()
    else:
        for z in range(planes):
            for copy in copies[z]:
                copy.start()
            pltpu.make_async_copy(
                f_hbm.at[pl.ds(z * rows, rows)], frc.at[pl.ds(z * rows, rows)], fload.at[z]
            ).start()
    zero = jnp.zeros((rows + 2 * PAD, cols), jnp.float32)
    for at in (0, planes + 1):
        vv[at] = zero
        uz[at] = zero[:rows]
        for c in range(3):
            adj[c, at] = zero
    inner = [
        (gx > 0).astype(jnp.float32),
        (gx < n_gx - 1).astype(jnp.float32),
        (gy > 0).astype(jnp.float32),
        (gy < n_gy - 1).astype(jnp.float32),
    ]
    lanes = lane_iota(rows)
    for side in range(2):
        packed = yh_ref[side] * inner[2 + side]
        packed = jnp.where(lanes < 3 * planes, packed, packed * half_step)
        if not leading:
            packed = jnp.where(lanes < 3 * planes, ya_ref[side] * inner[2 + side], packed)
        yh[side] = packed
    ends = ((0, PAD - 1), (1, PAD + rows))

    def fields(z):
        ux[z + 1, PAD : PAD + rows, :] = vel[0, z].astype(jnp.float32) * half_step
        uy[z + 1] = vel[1, z].astype(jnp.float32) * half_step
        uz[z + 1] = vel[2, z].astype(jnp.float32) * half_step
        vv[z + 1, PAD : PAD + rows, :] = visc[z].astype(jnp.float32) * half_step
        for side, at in ends:
            ux[z + 1, at : at + 1, :] = xh_ref[side, pl.ds(3 * planes + z, 1), :] * (inner[side] * half_step)
            vv[z + 1, at : at + 1, :] = xh_ref[side, pl.ds(4 * planes + z, 1), :] * (inner[side] * half_step)
            for c in range(3):
                edge = (xh_ref if leading else xa_ref)[side, pl.ds(c * planes + z, 1), :]
                adj[c, z + 1, at : at + 1, :] = edge * inner[side]

    def arrive(z):
        pltpu.make_async_copy(visc_in.at[z], visc.at[z], load.at[1, z]).wait()
        pltpu.make_async_copy(adj_in.at[:, z], adj.at[:, z + 1, pl.ds(PAD, rows), :], load.at[2, z]).wait()
        if not leading:
            pltpu.make_async_copy(vel_in.at[:, z], vel.at[:, z], load.at[0, z]).wait()

    if leading:
        xe_ref[...] = jnp.zeros_like(xe_ref)
        ye_ref[...] = jnp.zeros_like(ye_ref)
        for z in range(planes):
            copies[z][0].wait()
        line_forcing(recv_in, vel, weight_ref, high, low)
        place_lines(recv_in, high, low, frc)
        whole = pltpu.make_async_copy(frc, f_hbm, fsave)
        whole.start()
    arrive(0)
    fields(0)

    @pl.loop(0, planes)
    def _(z):
        @pl.when(z + 1 < planes)
        def _():
            arrive(z + 1)
            fields(z + 1)

        if not leading:
            pltpu.make_async_copy(
                f_hbm.at[pl.ds(z * rows, rows)], frc.at[pl.ds(z * rows, rows)], fload.at[z]
            ).wait()

        def forcing(r, lane):
            return frc[pl.ds(z * rows + r * SUB, SUB), pl.ds(lane, LANES)]

        sweep_plane(
            z, planes, rows, adj, ux, uy, uz, vv, yh, forcing, out,
            xe_ref if leading else None, ye_ref if leading else None,
        )
        pltpu.make_async_copy(out.at[:, z], out_hbm.at[:, z], save.at[z]).start()

    for z in range(planes):
        pltpu.make_async_copy(out.at[:, z], out_hbm.at[:, z], save.at[z]).wait()
    if leading:
        whole.wait()


def sweep(leading, n_gx, n_gy, *arrays):
    visc = arrays[3 if leading else 2]
    planes, rows, cols = visc.shape
    f32, bf16 = jnp.float32, jnp.bfloat16
    vmem = pl.BlockSpec(memory_space=pltpu.VMEM)
    any_space = pl.BlockSpec(memory_space=pl.ANY)
    result = jax.ShapeDtypeStruct((3, planes, rows, cols), f32)
    dma = pltpu.SemaphoreType.DMA
    scratch = [
        pltpu.VMEM((3, planes, rows, cols), bf16),
        pltpu.VMEM((planes, rows, cols), bf16),
        pltpu.VMEM((3, planes + 2, rows + 2 * PAD, cols), f32),
        pltpu.VMEM((planes + 2, rows + 2 * PAD, cols), f32),
        pltpu.VMEM((planes + 2, rows, cols), f32),
        pltpu.VMEM((planes + 2, rows, cols), f32),
        pltpu.VMEM((planes + 2, rows + 2 * PAD, cols), f32),
        pltpu.VMEM((2, rows, LANES), f32),
        pltpu.VMEM((3, planes, rows, cols), f32),
        pltpu.VMEM((planes * rows, 3 * cols), f32),
    ]
    if leading:
        slots = arrays[0].shape[0]
        scratch += [
            pltpu.VMEM((slots, 3 * cols), bf16),
            pltpu.VMEM((slots, 3 * cols), bf16),
            dma((3, planes)),
            dma((planes,)),
            dma,
        ]
        in_specs = [vmem, vmem, any_space, any_space, any_space, vmem, vmem]
        out_specs = [any_space, any_space, vmem, vmem]
        out_shape = [
            result,
            jax.ShapeDtypeStruct((planes * rows, 3 * cols), f32),
            jax.ShapeDtypeStruct((2, 3 * planes, cols), f32),
            jax.ShapeDtypeStruct((2, rows, LANES), f32),
        ]
    else:
        scratch += [dma((3, planes)), dma((planes,)), dma((planes,))]
        in_specs = [any_space] * 4 + [vmem] * 4
        out_specs, out_shape = any_space, result
    return pl.pallas_call(
        functools.partial(sweep_kernel, n_gx, n_gy, leading),
        name="sweep_first" if leading else "sweep_second",
        in_specs=in_specs,
        out_specs=out_specs,
        out_shape=out_shape,
        scratch_shapes=scratch,
        compiler_params=pltpu.CompilerParams(vmem_limit_bytes=60 << 20),
    )(*arrays)


def local(
    n_gx,
    n_gy,
    velocity,
    kinetic_energy,
    dissipation_rate,
    adjoint_start,
    interp_weight,
    observed,
    window_weight,
    window_source,
    window_block,
    window_count,
):
    peers = n_gx * n_gy
    windows = window_block.shape[0]
    meta = jnp.stack([window_source[:, 0], window_block, window_count]).astype(jnp.float32)
    meta = jnp.concatenate([meta, window_weight[None], jnp.zeros((4, windows), jnp.float32)])
    slots, visc, xe, ye = prep(
        meta, observed, velocity, kinetic_energy, dissipation_rate, adjoint_start, peers
    )
    received, xh, yh = exchange(
        xe, ye, slots.reshape(peers, CAP, 4 * LANES), n_gx, n_gy, 0
    )
    received = received.reshape(peers * CAP, 4 * LANES)
    adjoint, forcing, xe, ye = sweep(
        True, n_gx, n_gy, received, interp_weight, velocity, visc, adjoint_start, xh, yh
    )
    xa, ya = exchange(xe, ye, None, n_gx, n_gy, 1)
    return sweep(False, n_gx, n_gy, forcing, velocity, visc, adjoint, xh, yh, xa, ya)


def solution(mesh):
    placed = (
        P(None, None, "gx", "gy"),
        P(None, "gx", "gy"),
        P(None, "gx", "gy"),
        P(None, None, "gx", "gy"),
        P(),
        P(None, ("gx", "gy"), None),
        P(("gx", "gy")),
        P(("gx", "gy"), None),
        P(("gx", "gy")),
        P(("gx", "gy")),
    )
    return jax.shard_map(
        functools.partial(local, mesh.shape["gx"], mesh.shape["gy"]),
        mesh=mesh,
        in_specs=placed,
        out_specs=P(None, None, "gx", "gy"),
        check_vma=False,
    )
```

time: 482 us -> 140 us (0.29)
  the two profiles are of different devices: /device:TPU:33 before, /device:TPU:1 now
where the time goes in v1:
time: 140 us; the launch traced here: 139 us
  Pallas kernels  123 us (88%)
  local copies, waits for them, and re-layouts  14.4 us (10%)
  other arithmetic  1.47 us (1%)
    pallas_call x2, Pallas kernels, sweep(): pl.pallas_call(functools.partial(sweep_kernel, n_gx, n_gy, leading), name...  81.1 us
    pallas_call x2, Pallas kernels, exchange(): pl.pallas_call(functools.partial(exchange_kernel, n_gx, n_gy, slots is no...  36.2 us
    unnamed x16, local copies, waits for them, and re-layouts  10.5 us
    pallas_call x1, Pallas kernels, prep(): pl.pallas_call(prep_kernel, name='prep', grid=(planes,), in_specs=[pl.Blo...  5.96 us

profile of v1, /device:TPU:1, one launch (start us, length us, event | category | flops | bytes accessed | tf_op | source)
XLA Modules:
  0.0 139.2 jit_solution(2026908218557396414)
XLA Ops:
  0.0 0.1 pad.2.clone
  0.1 0.7 add_convert_fusion
  0.8 0.7 maximum_maximum_fusion.meta_ref
  1.5 0.0 copy-start
  1.6 1.9 %copy-done = bf16[3,16,128,256]{3,2,1,0:T(8,128)(2,1)S(1)} copy-done((bf16[3,16,128,256]{3,2,1,0:T(8,128)(2,1)S(1)}, bf16[3,16,128,256]{3,2,1,0:T(8,128)(2,1)}, u32[]{:S(2)}) %copy-start) | copy-done | bytes 3145752
  3.4 0.0 copy-start.1
  3.4 2.8 %copy-done.1 = f32[3,16,128,256]{3,2,1,0:T(8,128)S(1)} copy-done((f32[3,16,128,256]{3,2,1,0:T(8,128)S(1)}, f32[3,16,128,256]{3,2,1,0:T(8,128)}, u32[]{:S(2)}) %copy-start.1) | copy-done | bytes 6291480
  6.2 0.0 copy-start.3
  6.2 1.2 copy-done.3
  7.5 0.0 copy-start.4
  7.5 1.2 copy-done.4
  8.7 0.0 copy-start.5
  8.7 1.0 copy-done.5
  9.7 6.0 %prep.1 = (f32[512,512]{1,0:T(8,128)S(1)}, bf16[16,128,256]{2,1,0:T(8,128)(2,1)S(1)}, f32[2,80,256]{2,1,0:T(8,128)S(1)}, f32[2,128,128]{2,1,0:T(8,128)S(1)}) custom-call(f32[8,256]{1,0:T(8,128)S(1)} %maximum_maximum_fusion.meta_ref, f32[3,256,128]{2,1,0:T(8,128)S(1)} %copy-done.5, bf16[3,16,128,256]{3,2,1,0:T(8,128)(2,1)S(1)} %copy-done, ...), custom_call_target="tpu_custom_call" | custom-call | tf_op jit(solution)/shard_map/prep/pallas_call | solution.py:107
  15.6 0.0 copy-start.2
  15.6 1.0 copy-done.2
  16.7 0.0 copy-start.6
  16.7 0.6 copy-done.6
  17.3 0.0 copy-start.7
  17.3 0.6 copy-done.7
  18.0 1.3 reshape.6.refs_0_
  19.3 27.9 %exchange_slots.1 = (f32[128,4,512]{2,1,0:T(4,128)}, f32[2,80,256]{2,1,0:T(8,128)}, f32[2,128,128]{2,1,0:T(8,128)}) custom-call(f32[128,4,512]{2,1,0:T(4,128)} %reshape.6.refs_0_, f32[2,80,256]{2,1,0:T(8,128)} %copy-done.6, f32[2,128,128]{2,1,0:T(8,128)} %copy-done.7), custom_call_target="tpu_custom_call" | custom-call | tf_op jit(solution)/shard_map/exchange_slots/pallas_call | solution.py:202
  47.2 2.6 %reshape.7.refs_0_ = f32[512,512]{1,0:T(8,128)} reshape(f32[128,4,512]{2,1,0:T(4,128)} %get-tuple-element.21) | data formatting | bytes 2097152 | tf_op jit(solution)/shard_map/reshape | solution.py:531
  49.7 65.2 %sweep_first.1 = (f32[3,16,128,256]{3,2,1,0:T(8,128)}, f32[2048,768]{1,0:T(8,128)}, f32[2,48,256]{2,1,0:T(8,128)}, f32[2,128,128]{2,1,0:T(8,128)}) custom-call(f32[512,512]{1,0:T(8,128)} %reshape.7.refs_0_, bf16[128,256]{1,0:T(8,128)(2,1)} %refs_1_.2, bf16[3,16,128,256]{3,2,1,0:T(8,128)(2,1)} %refs_1_.3, bf16[16,128,256]{2,1,0:T(8,128)(2,1)} %copy-done.2, ...), custom_call_target="tpu_custom_call" | custom-call | tf_op jit(solution)/shard_map/sweep_first/pallas_call | solution.py:496
  115.0 8.3 %exchange_edges.1 = (f32[2,48,256]{2,1,0:T(8,128)}, f32[2,128,128]{2,1,0:T(8,128)}) custom-call(f32[2,48,256]{2,1,0:T(8,128)} %get-tuple-element.27.refs_0_, f32[2,128,128]{2,1,0:T(8,128)} %get-tuple-element.28.refs_1_), custom_call_target="tpu_custom_call" | custom-call | tf_op jit(solution)/shard_map/exchange_edges/pallas_call | solution.py:202
  123.3 15.9 %sweep_second.1 = f32[3,16,128,256]{3,2,1,0:T(8,128)} custom-call(f32[2048,768]{1,0:T(8,128)} %get-tuple-element.25.refs_0_, bf16[3,16,128,256]{3,2,1,0:T(8,128)(2,1)} %refs_1_.3, bf16[16,128,256]{2,1,0:T(8,128)(2,1)} %copy-done.2, f32[3,16,128,256]{3,2,1,0:T(8,128)} %get-tuple-element.26.refs_3_, f32[2,80,256]{2,1,0:T(8,128)} %get-tuple-element.23.refs_5_.refs_4_, ...), custom_call_target="tpu_custom_call" | custom-call | tf_op jit(solution)/shard_map/sweep_second/pallas_call | solution.py:496
  (1 shorter events, 0.0 us)
Async XLA Ops:
  1.5 1.9 %copy-start = (bf16[3,16,128,256]{3,2,1,0:T(8,128)(2,1)S(1)}, bf16[3,16,128,256]{3,2,1,0:T(8,128)(2,1)}, u32[]{:S(2)}) copy-start(bf16[3,16,128,256]{3,2,1,0:T(8,128)(2,1)} %refs_1_.3) | copy-start | bytes 9437188
  3.4 2.8 %copy-start.1 = (f32[3,16,128,256]{3,2,1,0:T(8,128)S(1)}, f32[3,16,128,256]{3,2,1,0:T(8,128)}, u32[]{:S(2)}) copy-start(f32[3,16,128,256]{3,2,1,0:T(8,128)} %refs_4_.1) | copy-start | bytes 18874372
  6.2 1.2 copy-start.3
  7.5 1.2 copy-start.4
  8.7 1.0 copy-start.5
  15.6 1.1 copy-start.2
  16.7 0.7 copy-start.6
  17.3 0.7 copy-start.7

commit v2 on v0

v2 whole, which is shorter than its diff:
```python
import functools

import jax
import jax.numpy as jnp
from jax import lax
from jax.experimental import pallas as pl
from jax.experimental.pallas import tpu as pltpu
from jax.sharding import PartitionSpec as P

MESH = pl.DeviceIdType.MESH
SWEEPS = 2
CAP = 4
LANES = 128
SUB = 8

base_viscosity = 0.05
pseudo_step = 0.4
half_step = 0.5 * pseudo_step

HALF = 2 * LANES
BLOCK, COUNT, WEIGHT = 0, 1, 2
PAD = 8


def lane_iota(rows=SUB):
    return lax.broadcasted_iota(jnp.int32, (rows, LANES), 1)


def split(x, pieces):
    out = []
    for _ in range(pieces):
        piece = x.astype(jnp.bfloat16)
        out.append(piece)
        x = x - piece.astype(jnp.float32)
    return out


def fill_slots(source, block, count, weight, obs_ref, slots_ref):
    windows = source.shape[1]
    peers = slots_ref.shape[0]
    slots = peers * CAP
    f32 = jnp.float32
    meta = jnp.concatenate(
        [
            block.astype(f32),
            count.astype(f32),
            weight,
            source.astype(f32),
            jnp.zeros((LANES - 4, windows), f32),
        ],
        axis=0,
    ).T
    first = lax.broadcasted_iota(jnp.int32, (windows, windows), 0)
    second = lax.broadcasted_iota(jnp.int32, (windows, windows), 1)
    same = (meta[:, 3:4] == source.astype(f32)) & (first < second)
    place = jnp.sum(same.astype(f32), axis=0, keepdims=True).astype(jnp.int32)
    chosen = lax.broadcasted_iota(jnp.int32, (slots, windows), 0) == source * CAP + place
    chosen = chosen.astype(jnp.bfloat16)
    top = lax.broadcasted_iota(jnp.int32, (slots // SUB, SUB, LANES), 1) < CAP
    quarters = []
    for values in (obs_ref[0], obs_ref[1], obs_ref[2], meta):
        total = jnp.zeros((slots, LANES), f32)
        for piece in reversed(split(values, 3)):
            total = total + jnp.dot(chosen, piece, preferred_element_type=f32)
        quarters.append(total.reshape(slots // SUB, SUB, LANES))
    for h in range(2):
        upper, lower = quarters[h], quarters[2 + h]
        even = jnp.where(top, upper, pltpu.roll(lower, CAP, axis=1))
        odd = jnp.where(top, pltpu.roll(upper, CAP, axis=1), lower)
        slots_ref[:, :, h * LANES : (h + 1) * LANES] = jnp.stack([even, odd], axis=1).reshape(
            peers, SUB, LANES
        )


def read_slots(recv_ref):
    peers = recv_ref.shape[0]
    top = lax.broadcasted_iota(jnp.int32, (peers // 2, SUB, LANES), 1) < CAP
    quarters = [None] * 4
    for h in range(2):
        pairs = recv_ref[:, :, h * LANES : (h + 1) * LANES].reshape(peers // 2, 2, SUB, LANES)
        even, odd = pairs[:, 0], pairs[:, 1]
        upper = jnp.where(top, even, pltpu.roll(odd, CAP, axis=1))
        lower = jnp.where(top, pltpu.roll(even, CAP, axis=1), odd)
        quarters[h] = upper.reshape(peers * CAP, LANES)
        quarters[2 + h] = lower.reshape(peers * CAP, LANES)
    return quarters


def line_forcing(quarters, vel_ref, weight_ref, high_ref, low_ref):
    meta = quarters[3]
    slots = meta.shape[0]
    planes, rows, cols = vel_ref.shape[1:]
    weights = weight_ref[...]
    block = meta[:, BLOCK : BLOCK + 1].astype(jnp.int32)
    count = meta[:, COUNT : COUNT + 1].astype(jnp.int32)
    scale = meta[:, WEIGHT : WEIGHT + 1]
    inside = lax.broadcasted_iota(jnp.int32, (slots, cols), 1) < count
    group = 4
    lines = [jnp.zeros((slots, cols), jnp.float32) for _ in range(3)]
    for q in range(planes // group):
        number = lax.broadcasted_iota(jnp.int32, (slots, group * rows), 1) + q * group * rows
        chosen = (number == block).astype(jnp.bfloat16)
        for c in range(3):
            some = vel_ref[c, q * group : (q + 1) * group].reshape(group * rows, cols)
            lines[c] = lines[c] + jnp.dot(chosen, some, preferred_element_type=jnp.float32)
    for c in range(3):
        masked = jnp.where(inside, lines[c], 0.0).astype(jnp.bfloat16)
        predicted = lax.dot_general(
            masked, weights, (((1,), (1,)), ((), ())), preferred_element_type=jnp.float32
        )
        high, low = split(scale * (predicted - quarters[c]), 2)
        placed = jnp.dot(low, weights, preferred_element_type=jnp.float32)
        placed = placed + jnp.dot(high, weights, preferred_element_type=jnp.float32)
        high, low = split(jnp.where(inside, pseudo_step * placed, 0.0), 2)
        high_ref[:, c * cols : (c + 1) * cols] = high
        low_ref[:, c * cols : (c + 1) * cols] = low


GROUP = 4


def place_lines(q, block, high_ref, low_ref, forcing, out):
    slots = high_ref.shape[0]
    rows, cols = forcing.shape[2:]
    step = GROUP * rows
    number = lax.broadcasted_iota(jnp.int32, (step, slots), 0) + q * step
    chosen = (number == block).astype(jnp.bfloat16)
    at = slice(q * GROUP, (q + 1) * GROUP)
    for c in range(3):
        lanes = slice(c * cols, (c + 1) * cols)
        total = jnp.dot(chosen, low_ref[:, lanes], preferred_element_type=jnp.float32)
        total = total + jnp.dot(chosen, high_ref[:, lanes], preferred_element_type=jnp.float32)
        total = total.reshape(GROUP, rows, cols)
        forcing[c, at] = total
        out[c, at] = out[c, at] + total


def pack_edges(fields_x, fields_y, rows, cols, xe, ye):
    for k, read in enumerate(fields_x):
        xe[0, k : k + 1, :] = read(slice(0, 1), slice(0, cols))
        xe[1, k : k + 1, :] = read(slice(rows - 1, rows), slice(0, cols))
    lanes = lane_iota()

    @pl.loop(0, rows // SUB)
    def _(r):
        base = pl.multiple_of(r * SUB, SUB)
        low = jnp.zeros((SUB, LANES), jnp.float32)
        high = jnp.zeros((SUB, LANES), jnp.float32)
        for k, read in enumerate(fields_y):
            here = lanes == k
            first = pltpu.roll(read(pl.ds(base, SUB), slice(0, LANES)), k, axis=1)
            last = pltpu.roll(read(pl.ds(base, SUB), slice(cols - LANES, cols)), (k + 1) % LANES, axis=1)
            low = jnp.where(here, first, low)
            high = jnp.where(here, last, high)
        ye[0, pl.ds(base, SUB), :] = low
        ye[1, pl.ds(base, SUB), :] = high


def inside_flags(n_gx, n_gy):
    gx, gy = lax.axis_index("gx"), lax.axis_index("gy")
    flags = (gx > 0, gx < n_gx - 1, gy > 0, gy < n_gy - 1)
    return [flag.astype(jnp.float32) for flag in flags]


def shifted(rows, by):
    if isinstance(rows, slice):
        return slice(rows.start + by, rows.stop + by)
    return pl.ds(pl.multiple_of(rows.start + by, SUB), rows.size)


def clear_outside(planes, rows, cols, adj, uz, vv):
    zero = jnp.zeros((rows, cols), jnp.float32)
    for at in (0, planes + 1):
        vv[at, PAD : PAD + rows, :] = zero
        uz[at] = zero
        for c in range(3):
            adj[c, at, PAD : PAD + rows, :] = zero


def up_down(pair, below, above, first, last):
    left, right = pair
    left_up, right_up = pltpu.roll(left, LANES - 1, axis=1), pltpu.roll(right, LANES - 1, axis=1)
    left_down, right_down = pltpu.roll(left, 1, axis=1), pltpu.roll(right, 1, axis=1)
    up = (jnp.where(last, right_up, left_up), jnp.where(last, above, right_up))
    down = (jnp.where(first, below, left_down), jnp.where(first, left_down, right_down))
    return up, down


def sweep_plane(z, planes, rows, adj, ux, uy, uz, vv, yh, forcing, out):
    lanes = lane_iota()
    first, last = lanes == 0, lanes == LANES - 1
    here = z + 1

    def pair(ref, *index):
        return ref[(*index, slice(0, LANES))], ref[(*index, slice(LANES, 2 * LANES))]

    for r in range(rows // SUB):
        at = slice(r * SUB, (r + 1) * SUB)
        mid = slice(PAD + r * SUB, PAD + (r + 1) * SUB)
        plus = slice(PAD + r * SUB + 1, PAD + (r + 1) * SUB + 1)
        minus = slice(PAD + r * SUB - 1, PAD + (r + 1) * SUB - 1)
        edge_low, edge_high = yh[0, at, :], yh[1, at, :]

        def outside(k):
            lane = k * planes + z
            return (
                pltpu.roll(edge_low, LANES - lane, axis=1),
                pltpu.roll(edge_high, LANES - 1 - lane, axis=1),
            )

        v = pair(vv, here, mid)
        v_xp, v_xm = pair(vv, here, plus), pair(vv, here, minus)
        v_zp, v_zm = pair(vv, here + 1, mid), pair(vv, here - 1, mid)
        v_yp, v_ym = up_down(v, *outside(4), first, last)
        u_xp, u_xm = pair(ux, here, plus), pair(ux, here, minus)
        u_yp, u_ym = up_down(pair(uy, here, at), *outside(3), first, last)
        u_zp, u_zm = pair(uz, here + 1, at), pair(uz, here - 1, at)
        coef = []
        for h in range(2):
            n = [v[h] + w[h] for w in (v_xp, v_xm, v_yp, v_ym, v_zp, v_zm)]
            centre = 1.0 - ((n[0] + n[1]) + (n[2] + n[3]) + (n[4] + n[5]))
            coef.append(
                (
                    centre,
                    n[0] - u_xp[h],
                    n[1] + u_xm[h],
                    n[2] - u_yp[h],
                    n[3] + u_ym[h],
                    n[4] - u_zp[h],
                    n[5] + u_zm[h],
                )
            )
        for c in range(3):
            a = pair(adj, c, here, mid)
            a_xp, a_xm = pair(adj, c, here, plus), pair(adj, c, here, minus)
            a_zp, a_zm = pair(adj, c, here + 1, mid), pair(adj, c, here - 1, mid)
            a_yp, a_ym = up_down(a, *outside(c), first, last)
            for h in range(2):
                k = coef[h]
                value = k[0] * a[h] + (k[1] * a_xp[h] + k[2] * a_xm[h])
                value = value + (k[3] * a_yp[h] + k[4] * a_ym[h])
                value = value + (k[5] * a_zp[h] + k[6] * a_zm[h])
                half = slice(h * LANES, (h + 1) * LANES)
                if forcing is not None:
                    value = value + forcing[c, z, at, half]
                out[c, z, at, half] = value


def first_kernel(n_gx, n_gy, *refs):
    (source, block, count, weight, obs, weights, vel_in, ke_in, dr_in, adj_in,
     out_hbm, f_hbm, visc_hbm, xh, yh, xa, ya,
     slots, recv, vel, ke, dr, visc, adj, ux, uy, uz, vv, yhs, out, frc, high, low, xe, ye, xe2, ye2,
     load, save, all_send, all_recv, local_sem, send, received) = refs
    planes, rows, cols = visc.shape
    peers = n_gx * n_gy
    gx, gy = lax.axis_index("gx"), lax.axis_index("gy")
    me = gx * n_gy + gy

    def device(step):
        peer = lax.rem(me + step, peers)
        return peer, (peer // n_gy, lax.rem(peer, n_gy))

    lower_x = (lax.rem(gx + n_gx - 1, n_gx), gy)
    upper_x = (lax.rem(gx + 1, n_gx), gy)
    lower_y = (gx, lax.rem(gy + n_gy - 1, n_gy))
    upper_y = (gx, lax.rem(gy + 1, n_gy))

    def edge_copies(turn, x_from, y_from, x_to, y_to):
        sides = (
            (x_from.at[1], x_to.at[0], upper_x),
            (x_from.at[0], x_to.at[1], lower_x),
            (y_from.at[1], y_to.at[0], upper_y),
            (y_from.at[0], y_to.at[1], lower_y),
        )
        return [
            pltpu.make_async_remote_copy(
                here, there, send.at[turn, k], received.at[turn, k], device_id=where, device_id_type=MESH
            )
            for k, (here, there, where) in enumerate(sides)
        ]

    adj_inner = adj.at[:, pl.ds(1, planes), pl.ds(PAD, rows), :]
    loads = [
        pltpu.make_async_copy(ke_in, ke, load.at[0]),
        pltpu.make_async_copy(dr_in, dr, load.at[1]),
        pltpu.make_async_copy(vel_in, vel, load.at[2]),
        pltpu.make_async_copy(adj_in, adj_inner, load.at[3]),
    ]
    for copy in loads:
        copy.start()
    barrier = pltpu.get_barrier_semaphore()

    @pl.loop(1, peers)
    def _(step):
        pl.semaphore_signal(barrier, inc=1, device_id=device(step)[1], device_id_type=MESH)

    fill_slots(source[...], block[...], count[...], weight[...], obs, slots)
    pl.semaphore_wait(barrier, peers - 1)
    own = pltpu.make_async_copy(slots.at[me], recv.at[me], local_sem)
    own.start()

    @pl.loop(1, peers)
    def _(step):
        peer, where = device(step)
        pltpu.make_async_remote_copy(
            slots.at[peer], recv.at[me], all_send, all_recv, device_id=where, device_id_type=MESH
        ).start()

    clear_outside(planes, rows, cols, adj, uz, vv)
    for copy in loads[:3]:
        copy.wait()

    @pl.loop(0, planes)
    def _(z):
        value = base_viscosity + ke[z].astype(jnp.float32) / dr[z].astype(jnp.float32)
        value = value.astype(jnp.bfloat16)
        visc[z] = value
        vv[z + 1, PAD : PAD + rows, :] = value.astype(jnp.float32) * half_step
        ux[z + 1, PAD : PAD + rows, :] = vel[0, z].astype(jnp.float32) * half_step
        uy[z + 1] = vel[1, z].astype(jnp.float32) * half_step
        uz[z + 1] = vel[2, z].astype(jnp.float32) * half_step

    visc_save = pltpu.make_async_copy(visc, visc_hbm, save.at[8])
    visc_save.start()
    loads[3].wait()

    def of_adj(c, z):
        return lambda at, lanes: adj[c, z + 1, shifted(at, PAD), lanes]

    def padded(ref, z):
        return lambda at, lanes: ref[z + 1, shifted(at, PAD), lanes]

    def of_uy(z):
        return lambda at, lanes: uy[z + 1, at, lanes]

    starts = [of_adj(c, z) for c in range(3) for z in range(planes)]
    visc_fields = [padded(vv, z) for z in range(planes)]
    pack_edges(
        starts + [padded(ux, z) for z in range(planes)] + visc_fields,
        starts + [of_uy(z) for z in range(planes)] + visc_fields,
        rows, cols, xe, ye,
    )
    copies = edge_copies(0, xe, ye, xh, yh)
    for copy in copies:
        copy.start()
    for copy in copies:
        copy.wait()
    inner = inside_flags(n_gx, n_gy)
    for side, at in ((0, PAD - 1), (1, PAD + rows)):
        for z in range(planes):
            for c in range(3):
                k = c * planes + z
                adj[c, z + 1, at : at + 1, :] = xh[side, k : k + 1, :] * inner[side]
            k = 3 * planes + z
            ux[z + 1, at : at + 1, :] = xh[side, k : k + 1, :] * inner[side]
            k = 4 * planes + z
            vv[z + 1, at : at + 1, :] = xh[side, k : k + 1, :] * inner[side]
        yhs[side] = yh[side] * inner[2 + side]

    @pl.loop(0, planes)
    def _(z):
        sweep_plane(z, planes, rows, adj, ux, uy, uz, vv, yhs, None, out)

    own.wait()
    rest = pl.ds(0, peers - 1)
    pltpu.make_async_copy(slots.at[rest], slots.at[rest], all_send).wait()
    pltpu.make_async_copy(recv.at[rest], recv.at[rest], all_recv).wait()
    quarters = read_slots(recv)
    line_forcing(quarters, vel, weights, high, low)
    line_row = quarters[3].T[BLOCK : BLOCK + 1].astype(jnp.int32)
    saves = []
    for q in range(planes // GROUP):
        place_lines(q, line_row, high, low, frc, out)
        at = pl.ds(q * GROUP, GROUP)
        saves.append(pltpu.make_async_copy(frc.at[:, at], f_hbm.at[:, at], save.at[2 * q]))
        saves.append(pltpu.make_async_copy(out.at[:, at], out_hbm.at[:, at], save.at[2 * q + 1]))
        for copy in saves[-2:]:
            copy.start()

    def of_out(c, z):
        return lambda at, lanes: out[c, z, at, lanes]

    news = [of_out(c, z) for c in range(3) for z in range(planes)]
    pack_edges(news, news, rows, cols, xe2, ye2)
    copies = edge_copies(1, xe2, ye2, xa, ya)
    for copy in copies:
        copy.start()
    for copy in copies:
        copy.wait()
    for copy in saves:
        copy.wait()
    visc_save.wait()


def second_kernel(n_gx, n_gy, starts, *refs):
    (f_in, vel_in, visc_in, adj_in, xh, yh, xa, ya,
     out_hbm,
     vel, visc, adj, ux, uy, uz, vv, yhs, out, frc, load, save) = refs
    planes, rows, cols = visc.shape
    ends = starts[1:] + (planes,)

    def group(g):
        here = pl.ds(starts[g], ends[g] - starts[g])
        there = pl.ds(starts[g] + 1, ends[g] - starts[g])
        return [
            pltpu.make_async_copy(vel_in.at[:, here], vel.at[:, here], load.at[0, g]),
            pltpu.make_async_copy(visc_in.at[here], visc.at[here], load.at[1, g]),
            pltpu.make_async_copy(adj_in.at[:, here], adj.at[:, there, pl.ds(PAD, rows), :], load.at[2, g]),
            pltpu.make_async_copy(f_in.at[:, here], frc.at[:, here], load.at[3, g]),
        ]

    groups = [group(g) for g in range(len(starts))]
    for copies in groups:
        for copy in copies:
            copy.start()
    clear_outside(planes, rows, cols, adj, uz, vv)
    inner = inside_flags(n_gx, n_gy)
    lanes = lane_iota(rows)
    for side, at in ((0, PAD - 1), (1, PAD + rows)):
        for z in range(planes):
            for c in range(3):
                k = c * planes + z
                adj[c, z + 1, at : at + 1, :] = xa[side, k : k + 1, :] * inner[side]
            k = 3 * planes + z
            ux[z + 1, at : at + 1, :] = xh[side, k : k + 1, :] * inner[side]
            k = 4 * planes + z
            vv[z + 1, at : at + 1, :] = xh[side, k : k + 1, :] * inner[side]
        yhs[side] = jnp.where(lanes < 3 * planes, ya[side], yh[side]) * inner[2 + side]

    def fields(z):
        ux[z + 1, PAD : PAD + rows, :] = vel[0, z].astype(jnp.float32) * half_step
        uy[z + 1] = vel[1, z].astype(jnp.float32) * half_step
        uz[z + 1] = vel[2, z].astype(jnp.float32) * half_step
        vv[z + 1, PAD : PAD + rows, :] = visc[z].astype(jnp.float32) * half_step

    for copy in groups[0]:
        copy.wait()
    fields(0)

    @pl.loop(0, planes)
    def _(z):
        for g in range(1, len(starts)):

            @pl.when(z + 1 == starts[g])
            def _():
                for copy in groups[g]:
                    copy.wait()

        @pl.when(z + 1 < planes)
        def _():
            fields(z + 1)

        sweep_plane(z, planes, rows, adj, ux, uy, uz, vv, yhs, frc, out)
        pltpu.make_async_copy(out.at[:, z], out_hbm.at[:, z], save).start()

    pltpu.make_async_copy(out, out_hbm, save).wait()


def field_scratch(planes, rows, cols):
    f32, bf16 = jnp.float32, jnp.bfloat16
    tall = rows + 2 * PAD
    return [
        pltpu.VMEM((planes, rows, cols), bf16),
        pltpu.VMEM((3, planes + 2, tall, cols), f32),
        pltpu.VMEM((planes + 2, tall, cols), f32),
        pltpu.VMEM((planes + 2, rows, cols), f32),
        pltpu.VMEM((planes + 2, rows, cols), f32),
        pltpu.VMEM((planes + 2, tall, cols), f32),
        pltpu.VMEM((2, rows, LANES), f32),
        pltpu.VMEM((3, planes, rows, cols), f32),
        pltpu.VMEM((3, planes, rows, cols), f32),
    ]


def local(
    n_gx,
    n_gy,
    velocity,
    kinetic_energy,
    dissipation_rate,
    adjoint_start,
    interp_weight,
    observed,
    window_weight,
    window_source,
    window_block,
    window_count,
):
    planes, rows, cols = kinetic_energy.shape
    peers = n_gx * n_gy
    windows = window_block.shape[0]
    f32, bf16 = jnp.float32, jnp.bfloat16
    shape = jax.ShapeDtypeStruct
    vmem = pl.BlockSpec(memory_space=pltpu.VMEM)
    hbm = pl.BlockSpec(memory_space=pl.ANY)
    dma = pltpu.SemaphoreType.DMA
    whole = shape(adjoint_start.shape, f32)
    edges = [
        shape((2, 5 * planes, cols), f32),
        shape((2, rows, LANES), f32),
        shape((2, 3 * planes, cols), f32),
        shape((2, rows, LANES), f32),
    ]
    flat = (1, windows)
    adjoint, forcing, visc, xh, yh, xa, ya = pl.pallas_call(
        functools.partial(first_kernel, n_gx, n_gy),
        name="route_and_first_sweep",
        in_specs=[vmem] * 6 + [hbm] * 4,
        out_specs=[hbm] * 3 + [vmem] * 4,
        out_shape=[whole, whole, shape((planes, rows, cols), bf16)] + edges,
        scratch_shapes=[
            pltpu.VMEM((peers, SUB, HALF), f32),
            pltpu.VMEM((peers, SUB, HALF), f32),
            pltpu.VMEM((3, planes, rows, cols), bf16),
            pltpu.VMEM((planes, rows, cols), bf16),
            pltpu.VMEM((planes, rows, cols), bf16),
        ]
        + field_scratch(planes, rows, cols)
        + [
            pltpu.VMEM((peers * CAP, 3 * cols), bf16),
            pltpu.VMEM((peers * CAP, 3 * cols), bf16),
        ]
        + [pltpu.VMEM(e.shape, e.dtype) for e in edges]
        + [dma((4,)), dma((2 * planes // GROUP + 1,)), dma, dma, dma, dma((2, 4)), dma((2, 4))],
        compiler_params=pltpu.CompilerParams(
            collective_id=0, has_side_effects=True, vmem_limit_bytes=60 << 20
        ),
    )(
        window_source.reshape(flat),
        window_block.reshape(flat),
        window_count.reshape(flat),
        window_weight.reshape(flat),
        observed,
        interp_weight,
        velocity,
        kinetic_energy,
        dissipation_rate,
        adjoint_start,
    )
    starts = (0, 1, 2, 4, 8, 12)
    return pl.pallas_call(
        functools.partial(second_kernel, n_gx, n_gy, starts),
        name="second_sweep",
        in_specs=[hbm] * 4 + [vmem] * 4,
        out_specs=hbm,
        out_shape=whole,
        scratch_shapes=[pltpu.VMEM((3, planes, rows, cols), bf16)]
        + field_scratch(planes, rows, cols)
        + [dma((4, len(starts))), dma],
        compiler_params=pltpu.CompilerParams(vmem_limit_bytes=60 << 20),
    )(forcing, velocity, visc, adjoint, xh, yh, xa, ya)


def solution(mesh):
    placed = (
        P(None, None, "gx", "gy"),
        P(None, "gx", "gy"),
        P(None, "gx", "gy"),
        P(None, None, "gx", "gy"),
        P(),
        P(None, ("gx", "gy"), None),
        P(("gx", "gy")),
        P(("gx", "gy"), None),
        P(("gx", "gy")),
        P(("gx", "gy")),
    )
    return jax.shard_map(
        functools.partial(local, mesh.shape["gx"], mesh.shape["gy"]),
        mesh=mesh,
        in_specs=placed,
        out_specs=P(None, None, "gx", "gy"),
        check_vma=False,
    )
```

time: 482 us -> 69.4 us (0.14)
  the two profiles are of different devices: /device:TPU:33 before, /device:TPU:1 now
where the time goes in v2:
time: 69.4 us; the launch traced here: 69.1 us
  Pallas kernels  69.1 us (100%)
    pallas_call x1, Pallas kernels, local(): pl.pallas_call(functools.partial(first_kernel, n_gx, n_gy), name='route_a...  55.1 us
    pallas_call x1, Pallas kernels, local(): pl.pallas_call(functools.partial(second_kernel, n_gx, n_gy, starts), name...  14 us

profile of v2, /device:TPU:1, one launch (start us, length us, event | category | flops | bytes accessed | tf_op | source)
XLA Modules:
  0.0 69.1 jit_solution(6868693732595055574)
XLA Ops:
  0.0 55.1 %route_and_first_sweep.1 = (f32[3,16,128,256]{3,2,1,0:T(8,128)}, f32[3,16,128,256]{3,2,1,0:T(8,128)}, bf16[16,128,256]{2,1,0:T(8,128)(2,1)}, f32[2,80,256]{2,1,0...) custom-call(s32[1,256]{1,0:T(1,128)} %bitcast.4, s32[1,256]{1,0:T(1,128)} %bitcast.5, ...), custom_call_target="tpu_custom_call" | custom-call | tf_op jit(solution)/shard_map/route_and_first_sweep/pallas_call | solution.py:505
  55.1 14.0 %second_sweep.1 = f32[3,16,128,256]{3,2,1,0:T(8,128)} custom-call(f32[3,16,128,256]{3,2,1,0:T(8,128)} %get-tuple-element.12.refs_0_, bf16[3,16,128,256]{3,2,1,0:T(8,128)(2,1)} %refs_1_.1, bf16[16,128,256]{2,1,0:T(8,128)(2,1)} %get-tuple-element.13.refs_2_, f32[3,16,128,256]{3,2,1,0:T(8,128)} %get-tuple-element.14.refs_3_, ...), custom_call_target="tpu_custom_call" | custom-call | tf_op jit(solution)/shard_map/second_sweep/pallas_call | solution.py:541

commit v3 on v2

v3 whole, which is shorter than its diff:
```python
import functools

import jax
import jax.numpy as jnp
from jax import lax
from jax.experimental import pallas as pl
from jax.experimental.pallas import tpu as pltpu
from jax.sharding import PartitionSpec as P

MESH = pl.DeviceIdType.MESH
SWEEPS = 2
CAP = 4
LANES = 128
SUB = 8

base_viscosity = 0.05
pseudo_step = 0.4
half_step = 0.5 * pseudo_step

HALF = 2 * LANES
BLOCK, COUNT, WEIGHT = 0, 1, 2
PAD = 8


def lane_iota(rows=SUB):
    return lax.broadcasted_iota(jnp.int32, (rows, LANES), 1)


def split(x, pieces):
    out = []
    for _ in range(pieces):
        piece = x.astype(jnp.bfloat16)
        out.append(piece)
        x = x - piece.astype(jnp.float32)
    return out


def fill_slots(source, block, count, weight, obs_ref, slots_ref):
    windows = source.shape[1]
    peers = slots_ref.shape[0]
    slots = peers * CAP
    f32 = jnp.float32
    meta = jnp.concatenate(
        [
            block.astype(f32),
            count.astype(f32),
            weight,
            source.astype(f32),
            jnp.zeros((LANES - 4, windows), f32),
        ],
        axis=0,
    ).T
    first = lax.broadcasted_iota(jnp.int32, (windows, windows), 0)
    second = lax.broadcasted_iota(jnp.int32, (windows, windows), 1)
    same = (meta[:, 3:4] == source.astype(f32)) & (first < second)
    place = jnp.sum(same.astype(f32), axis=0, keepdims=True).astype(jnp.int32)
    chosen = lax.broadcasted_iota(jnp.int32, (slots, windows), 0) == source * CAP + place
    chosen = chosen.astype(jnp.bfloat16)
    top = lax.broadcasted_iota(jnp.int32, (slots // SUB, SUB, LANES), 1) < CAP
    quarters = []
    for values in (obs_ref[0], obs_ref[1], obs_ref[2], meta):
        total = jnp.zeros((slots, LANES), f32)
        for piece in reversed(split(values, 3)):
            total = total + jnp.dot(chosen, piece, preferred_element_type=f32)
        quarters.append(total.reshape(slots // SUB, SUB, LANES))
    for h in range(2):
        upper, lower = quarters[h], quarters[2 + h]
        even = jnp.where(top, upper, pltpu.roll(lower, CAP, axis=1))
        odd = jnp.where(top, pltpu.roll(upper, CAP, axis=1), lower)
        slots_ref[:, :, h * LANES : (h + 1) * LANES] = jnp.stack([even, odd], axis=1).reshape(
            peers, SUB, LANES
        )


def read_slots(recv_ref):
    peers = recv_ref.shape[0]
    top = lax.broadcasted_iota(jnp.int32, (peers // 2, SUB, LANES), 1) < CAP
    quarters = [None] * 4
    for h in range(2):
        pairs = recv_ref[:, :, h * LANES : (h + 1) * LANES].reshape(peers // 2, 2, SUB, LANES)
        even, odd = pairs[:, 0], pairs[:, 1]
        upper = jnp.where(top, even, pltpu.roll(odd, CAP, axis=1))
        lower = jnp.where(top, pltpu.roll(even, CAP, axis=1), odd)
        quarters[h] = upper.reshape(peers * CAP, LANES)
        quarters[2 + h] = lower.reshape(peers * CAP, LANES)
    return quarters


def line_forcing(quarters, vel_ref, weight_ref, high_ref, low_ref):
    meta = quarters[3]
    slots = meta.shape[0]
    planes, rows, cols = vel_ref.shape[1:]
    weights = weight_ref[...]
    block = meta[:, BLOCK : BLOCK + 1].astype(jnp.int32)
    count = meta[:, COUNT : COUNT + 1].astype(jnp.int32)
    scale = meta[:, WEIGHT : WEIGHT + 1]
    inside = lax.broadcasted_iota(jnp.int32, (slots, cols), 1) < count
    group = 4
    lines = [jnp.zeros((slots, cols), jnp.float32) for _ in range(3)]
    for q in range(planes // group):
        number = lax.broadcasted_iota(jnp.int32, (slots, group * rows), 1) + q * group * rows
        chosen = (number == block).astype(jnp.bfloat16)
        for c in range(3):
            some = vel_ref[c, q * group : (q + 1) * group].reshape(group * rows, cols)
            lines[c] = lines[c] + jnp.dot(chosen, some, preferred_element_type=jnp.float32)
    edge_values = []
    for c in range(3):
        masked = jnp.where(inside, lines[c], 0.0).astype(jnp.bfloat16)
        predicted = lax.dot_general(
            masked, weights, (((1,), (1,)), ((), ())), preferred_element_type=jnp.float32
        )
        high, low = split(scale * (predicted - quarters[c]), 2)
        placed = jnp.dot(low, weights, preferred_element_type=jnp.float32)
        placed = placed + jnp.dot(high, weights, preferred_element_type=jnp.float32)
        placed = jnp.where(inside, pseudo_step * placed, 0.0)
        edge_values.append((placed[:, 0:1], placed[:, cols - 1 : cols]))
        high, low = split(placed, 2)
        high_ref[:, c * cols : (c + 1) * cols] = high
        low_ref[:, c * cols : (c + 1) * cols] = low
    return edge_values


def force_edges(block, meta, edge_values, high_ref, low_ref, planes, rows, xe, ye):
    f32, bf16 = jnp.float32, jnp.bfloat16
    slots, width = high_ref.shape
    cols = width // 3
    number = lax.broadcasted_iota(jnp.int32, (2 * planes, slots), 0)
    line = number % planes * rows + number // planes * (rows - 1)
    chosen = (line == block).astype(bf16)
    total = jnp.dot(chosen, low_ref[...], preferred_element_type=f32)
    total = total + jnp.dot(chosen, high_ref[...], preferred_element_type=f32)
    for side in range(2):
        for c in range(3):
            at = slice(c * planes, (c + 1) * planes)
            xe[side, at, :] = xe[side, at, :] + total[side * planes : (side + 1) * planes, c * cols : (c + 1) * cols]
    lanes = lane_iota(slots)
    plane = meta[:, BLOCK : BLOCK + 1].astype(jnp.int32) // rows
    values = jnp.zeros((slots, LANES), f32)
    for c in range(3):
        for side in range(2):
            values = jnp.where(lanes // (2 * planes) * 2 + (1 - lanes % 2) == 2 * c + side, edge_values[c][side], values)
    values = jnp.where((lanes // 2 % planes == plane) & (lanes < 6 * planes), values, 0.0)
    chosen = (lax.broadcasted_iota(jnp.int32, (rows, slots), 0) == block % rows).astype(bf16)
    total = ye[...]
    for piece in reversed(split(values, 2)):
        total = total + jnp.dot(chosen, piece, preferred_element_type=f32)
    ye[...] = total


GROUP = 4


def place_lines(q, block, high_ref, low_ref, forcing, out):
    slots = high_ref.shape[0]
    rows, cols = forcing.shape[2:]
    step = GROUP * rows
    number = lax.broadcasted_iota(jnp.int32, (step, slots), 0) + q * step
    chosen = (number == block).astype(jnp.bfloat16)
    at = slice(q * GROUP, (q + 1) * GROUP)
    for c in range(3):
        lanes = slice(c * cols, (c + 1) * cols)
        total = jnp.dot(chosen, low_ref[:, lanes], preferred_element_type=jnp.float32)
        total = total + jnp.dot(chosen, high_ref[:, lanes], preferred_element_type=jnp.float32)
        total = total.reshape(GROUP, rows, cols)
        forcing[c, at] = total
        out[c, at] = out[c, at] + total


def pack_rows(fields, rows, cols, xe):
    for k, read in enumerate(fields):
        for h in range(2):
            half = slice(h * LANES, (h + 1) * LANES)
            xe[0, k : k + 1, half] = read(slice(0, 1), h)
            xe[1, k : k + 1, half] = read(slice(rows - 1, rows), h)


def pack_columns(fields, rows, ye):
    lanes = lane_iota()

    @pl.loop(0, rows // SUB)
    def _(r):
        at = pl.ds(pl.multiple_of(r * SUB, SUB), SUB)
        packed = jnp.zeros((SUB, LANES), jnp.float32)
        for k, read in fields:
            ends = jnp.where(lanes == 0, read(at, 0), read(at, 1))
            ends = pltpu.roll(ends, (2 * k + 1) % LANES, axis=1)
            packed = jnp.where(lanes // 2 == k, ends, packed)
        ye[at, :] = packed


def from_sides(yh, index):
    inner = inside_flags(*index)
    below = pltpu.roll(yh[0], 1, axis=1) * inner[2]
    above = pltpu.roll(yh[1], LANES - 1, axis=1) * inner[3]
    return jnp.where(lane_iota(below.shape[0]) % 2 == 1, below, above)


def inside_flags(n_gx, n_gy):
    gx, gy = lax.axis_index("gx"), lax.axis_index("gy")
    flags = (gx > 0, gx < n_gx - 1, gy > 0, gy < n_gy - 1)
    return [flag.astype(jnp.float32) for flag in flags]


def shifted(rows, by):
    if isinstance(rows, slice):
        return slice(rows.start + by, rows.stop + by)
    return pl.ds(pl.multiple_of(rows.start + by, SUB), rows.size)


def clear_outside(planes, rows, cols, adj, uz, vv):
    zero = jnp.zeros((rows, cols), jnp.float32)
    for at in (0, planes + 1):
        uz[at] = zero
        for h in range(2):
            vv[at, h, PAD : PAD + rows, :] = zero[:, :LANES]
            for c in range(3):
                adj[c, at, h, PAD : PAD + rows, :] = zero[:, :LANES]


def set_fields(z, vel, visc, ux, uy, uz, vv):
    rows = visc.shape[1]
    uy[z + 1] = vel[1, z].astype(jnp.float32) * half_step
    uz[z + 1] = vel[2, z].astype(jnp.float32) * half_step
    for h in range(2):
        half = slice(h * LANES, (h + 1) * LANES)
        vv[z + 1, h, PAD : PAD + rows, :] = visc[z, :, half].astype(jnp.float32) * half_step
        ux[z + 1, h, PAD : PAD + rows, :] = vel[0, z, :, half].astype(jnp.float32) * half_step


def set_rows(planes, rows, index, xa, xh, adj, ux, vv):
    inner = inside_flags(*index)
    for side, at in ((0, PAD - 1), (1, PAD + rows)):
        for z in range(planes):
            for h in range(2):
                half = slice(h * LANES, (h + 1) * LANES)
                for c in range(3):
                    k = c * planes + z
                    adj[c, z + 1, h, at : at + 1, :] = xa[side, k : k + 1, half] * inner[side]
                k = 3 * planes + z
                ux[z + 1, h, at : at + 1, :] = xh[side, k : k + 1, half] * inner[side]
                k = 4 * planes + z
                vv[z + 1, h, at : at + 1, :] = xh[side, k : k + 1, half] * inner[side]


def up_down(pair, outer, first, last):
    left, right = pair
    left_up, right_up = (pltpu.roll(x, LANES - 1, axis=1) for x in pair)
    left_down, right_down = (pltpu.roll(x, 1, axis=1) for x in pair)
    up = (jnp.where(last, right_up, left_up), jnp.where(last, outer, right_up))
    down = (jnp.where(first, outer, left_down), jnp.where(first, left_down, right_down))
    return up, down


def sweep_plane(z, planes, rows, adj, ux, uy, uz, vv, yhs, forcing, out):
    lanes = lane_iota()
    first, last = lanes == 0, lanes == LANES - 1
    here = z + 1
    both = (slice(0, LANES), slice(LANES, 2 * LANES))

    for r in range(rows // SUB):
        at = slice(r * SUB, (r + 1) * SUB)
        mid, plus, minus = (slice(at.start + PAD + d, at.stop + PAD + d) for d in (0, 1, -1))
        edges = [yhs[0, at, :], yhs[1, at, :]]

        def outer(which, k):
            return pltpu.roll(edges[which], LANES - 1 - 2 * (k * planes + z), axis=1)

        v = [vv[here, h, mid, :] for h in range(2)]
        v_yp, v_ym = up_down(v, outer(0, 3), first, last)
        u_yp, u_ym = up_down([uy[here, at, half] for half in both], outer(1, 3), first, last)
        coef = []
        for h in range(2):
            n_xp, n_xm = v[h] + vv[here, h, plus, :], v[h] + vv[here, h, minus, :]
            n_yp, n_ym = v[h] + v_yp[h], v[h] + v_ym[h]
            n_zp, n_zm = v[h] + vv[here + 1, h, mid, :], v[h] + vv[here - 1, h, mid, :]
            coef.append(
                (
                    1.0 - ((n_xp + n_xm) + (n_yp + n_ym) + (n_zp + n_zm)),
                    n_xp - ux[here, h, plus, :],
                    n_xm + ux[here, h, minus, :],
                    n_yp - u_yp[h],
                    n_ym + u_ym[h],
                    n_zp - uz[here + 1, at, both[h]],
                    n_zm + uz[here - 1, at, both[h]],
                )
            )
        for c in range(3):
            a = [adj[c, here, h, mid, :] for h in range(2)]
            a_yp, a_ym = up_down(a, outer(0, c), first, last)
            for h in range(2):
                k = coef[h]
                value = k[0] * a[h] + (k[1] * adj[c, here, h, plus, :] + k[2] * adj[c, here, h, minus, :])
                value = value + (k[3] * a_yp[h] + k[4] * a_ym[h])
                value = value + (k[5] * adj[c, here + 1, h, mid, :] + k[6] * adj[c, here - 1, h, mid, :])
                if forcing is not None:
                    value = value + forcing[c, z, at, both[h]]
                out[c, z, at, both[h]] = value


def first_kernel(n_gx, n_gy, *refs):
    (source, block, count, weight, obs, weights, vel_in, ke_in, dr_in, adj_in,
     out_hbm, f_hbm, visc_hbm, xh, yc, xa, ya,
     slots, recv, vel, ke, dr, visc, adj, ux, uy, uz, vv, yhs, out, frc, high, low, xe, ye, yh, xe2, ye2,
     load, save, all_send, all_recv, local_sem, send, received) = refs
    planes, rows, cols = visc.shape
    peers = n_gx * n_gy
    gx, gy = lax.axis_index("gx"), lax.axis_index("gy")
    me = gx * n_gy + gy

    def device(step):
        peer = lax.rem(me + step, peers)
        return peer, (peer // n_gy, lax.rem(peer, n_gy))

    lower_x = (lax.rem(gx + n_gx - 1, n_gx), gy)
    upper_x = (lax.rem(gx + 1, n_gx), gy)
    lower_y = (gx, lax.rem(gy + n_gy - 1, n_gy))
    upper_y = (gx, lax.rem(gy + 1, n_gy))

    def edge_copies(turn, x_from, y_from, x_to, y_to):
        sides = (
            (x_from.at[1], x_to.at[0], upper_x),
            (x_from.at[0], x_to.at[1], lower_x),
            (y_from, y_to.at[0], upper_y),
            (y_from, y_to.at[1], lower_y),
        )
        return [
            pltpu.make_async_remote_copy(
                here, there, send.at[turn, k], received.at[turn, k], device_id=where, device_id_type=MESH
            )
            for k, (here, there, where) in enumerate(sides)
        ]

    loads = [
        pltpu.make_async_copy(ke_in, ke, load.at[0]),
        pltpu.make_async_copy(dr_in, dr, load.at[1]),
        pltpu.make_async_copy(vel_in, vel, load.at[2]),
    ] + [
        pltpu.make_async_copy(
            adj_in.at[:, :, :, pl.ds(h * LANES, LANES)],
            adj.at[:, pl.ds(1, planes), h, pl.ds(PAD, rows), :],
            load.at[3 + h],
        )
        for h in range(2)
    ]
    for copy in loads:
        copy.start()
    barrier = pltpu.get_barrier_semaphore()

    @pl.loop(1, peers)
    def _(step):
        pl.semaphore_signal(barrier, inc=1, device_id=device(step)[1], device_id_type=MESH)

    fill_slots(source[...], block[...], count[...], weight[...], obs, slots)
    clear_outside(planes, rows, cols, adj, uz, vv)
    for copy in loads[:3]:
        copy.wait()

    @pl.loop(0, planes)
    def _(z):
        value = base_viscosity + ke[z].astype(jnp.float32) / dr[z].astype(jnp.float32)
        visc[z] = value.astype(jnp.bfloat16)
        set_fields(z, vel, visc, ux, uy, uz, vv)

    visc_save = pltpu.make_async_copy(visc, visc_hbm, save.at[8])
    visc_save.start()
    for copy in loads[3:]:
        copy.wait()

    def of_adj(c, z):
        return lambda at, h: adj[c, z + 1, h, shifted(at, PAD), :]

    def of_tall(ref, z):
        return lambda at, h: ref[z + 1, h, shifted(at, PAD), :]

    def of_uy(z):
        return lambda at, h: uy[z + 1, at, slice(h * LANES, (h + 1) * LANES)]

    starts = [of_adj(c, z) for c in range(3) for z in range(planes)]
    visc_fields = [of_tall(vv, z) for z in range(planes)]
    pack_rows(starts + [of_tall(ux, z) for z in range(planes)] + visc_fields, rows, cols, xe)
    pack_columns(list(enumerate(starts + visc_fields)), rows, ye.at[0])
    pack_columns([(3 * planes + z, of_uy(z)) for z in range(planes)], rows, ye.at[1])

    pl.semaphore_wait(barrier, peers - 1)
    copies = edge_copies(0, xe, ye, xh, yh)
    for copy in copies:
        copy.start()
    own = pltpu.make_async_copy(slots.at[me], recv.at[me], local_sem)
    own.start()

    @pl.loop(1, peers)
    def _(step):
        peer, where = device(step)
        pltpu.make_async_remote_copy(
            slots.at[peer], recv.at[me], all_send, all_recv, device_id=where, device_id_type=MESH
        ).start()

    for copy in copies:
        copy.wait()
    index = (n_gx, n_gy)
    set_rows(planes, rows, index, xh, xh, adj, ux, vv)
    for k in range(2):
        sides = from_sides(yh.at[:, k], index)
        yc[k] = sides
        yhs[k] = sides

    @pl.loop(0, planes)
    def _(z):
        sweep_plane(z, planes, rows, adj, ux, uy, uz, vv, yhs, None, out)

    def of_out(c, z):
        return lambda at, h: out[c, z, at, slice(h * LANES, (h + 1) * LANES)]

    news = [of_out(c, z) for c in range(3) for z in range(planes)]
    pack_rows(news, rows, cols, xe2)
    pack_columns(list(enumerate(news)), rows, ye2)

    own.wait()
    rest = pl.ds(0, peers - 1)
    pltpu.make_async_copy(slots.at[rest], slots.at[rest], all_send).wait()
    pltpu.make_async_copy(recv.at[rest], recv.at[rest], all_recv).wait()
    quarters = read_slots(recv)
    edge_values = line_forcing(quarters, vel, weights, high, low)
    block = quarters[3].T[BLOCK : BLOCK + 1].astype(jnp.int32)
    force_edges(block, quarters[3], edge_values, high, low, planes, rows, xe2, ye2)
    copies = edge_copies(1, xe2, ye2, xa, ya)
    for copy in copies:
        copy.start()
    saves = []
    for q in range(planes // GROUP):
        place_lines(q, block, high, low, frc, out)
        at = pl.ds(q * GROUP, GROUP)
        saves.append(pltpu.make_async_copy(frc.at[:, at], f_hbm.at[:, at], save.at[2 * q]))
        saves.append(pltpu.make_async_copy(out.at[:, at], out_hbm.at[:, at], save.at[2 * q + 1]))
        for copy in saves[-2:]:
            copy.start()
    for copy in copies + saves:
        copy.wait()
    visc_save.wait()


def second_kernel(n_gx, n_gy, starts, *refs):
    (f_in, vel_in, visc_in, adj_in, xh, yc, xa, ya,
     out_hbm,
     vel, visc, adj, ux, uy, uz, vv, yhs, out, frc, load, save) = refs
    planes, rows, cols = visc.shape
    ends = starts[1:] + (planes,)

    def group(g):
        here = pl.ds(starts[g], ends[g] - starts[g])
        there = pl.ds(starts[g] + 1, ends[g] - starts[g])
        return [
            pltpu.make_async_copy(vel_in.at[:, here], vel.at[:, here], load.at[0, g]),
            pltpu.make_async_copy(visc_in.at[here], visc.at[here], load.at[1, g]),
            pltpu.make_async_copy(f_in.at[:, here], frc.at[:, here], load.at[2, g]),
        ] + [
            pltpu.make_async_copy(
                adj_in.at[:, here, :, pl.ds(h * LANES, LANES)],
                adj.at[:, there, h, pl.ds(PAD, rows), :],
                load.at[3 + h, g],
            )
            for h in range(2)
        ]

    groups = [group(g) for g in range(len(starts))]
    for copies in groups:
        for copy in copies:
            copy.start()
    clear_outside(planes, rows, cols, adj, uz, vv)
    index = (n_gx, n_gy)
    set_rows(planes, rows, index, xa, xh, adj, ux, vv)
    adjoint_lanes = lane_iota(rows) < 6 * planes
    yhs[0] = jnp.where(adjoint_lanes, from_sides(ya, index), yc[0])
    yhs[1] = yc[1]

    def fields(z):
        set_fields(z, vel, visc, ux, uy, uz, vv)

    for copy in groups[0]:
        copy.wait()
    fields(0)

    @pl.loop(0, planes)
    def _(z):
        for g in range(1, len(starts)):

            @pl.when(z + 1 == starts[g])
            def _():
                for copy in groups[g]:
                    copy.wait()

        @pl.when(z + 1 < planes)
        def _():
            fields(z + 1)

        sweep_plane(z, planes, rows, adj, ux, uy, uz, vv, yhs, frc, out)
        pltpu.make_async_copy(out.at[:, z], out_hbm.at[:, z], save).start()

    pltpu.make_async_copy(out, out_hbm, save).wait()


def field_scratch(planes, rows, cols):
    f32, bf16 = jnp.float32, jnp.bfloat16
    tall = rows + 2 * PAD
    return [
        pltpu.VMEM((planes, rows, cols), bf16),
        pltpu.VMEM((3, planes + 2, 2, tall, LANES), f32),
        pltpu.VMEM((planes + 2, 2, tall, LANES), f32),
        pltpu.VMEM((planes + 2, rows, cols), f32),
        pltpu.VMEM((planes + 2, rows, cols), f32),
        pltpu.VMEM((planes + 2, 2, tall, LANES), f32),
        pltpu.VMEM((2, rows, LANES), f32),
        pltpu.VMEM((3, planes, rows, cols), f32),
        pltpu.VMEM((3, planes, rows, cols), f32),
    ]


def local(
    n_gx,
    n_gy,
    velocity,
    kinetic_energy,
    dissipation_rate,
    adjoint_start,
    interp_weight,
    observed,
    window_weight,
    window_source,
    window_block,
    window_count,
):
    planes, rows, cols = kinetic_energy.shape
    peers = n_gx * n_gy
    windows = window_block.shape[0]
    f32, bf16 = jnp.float32, jnp.bfloat16
    shape = jax.ShapeDtypeStruct
    vmem = pl.BlockSpec(memory_space=pltpu.VMEM)
    hbm = pl.BlockSpec(memory_space=pl.ANY)
    dma = pltpu.SemaphoreType.DMA
    whole = shape(adjoint_start.shape, f32)
    sides = [
        shape((2, 5 * planes, cols), f32),
        shape((2, rows, LANES), f32),
        shape((2, 3 * planes, cols), f32),
        shape((2, rows, LANES), f32),
    ]
    edges = [
        (2, 5 * planes, cols),
        (2, rows, LANES),
        (2, 2, rows, LANES),
        (2, 3 * planes, cols),
        (rows, LANES),
    ]
    flat = (1, windows)
    adjoint, forcing, visc, xh, yc, xa, ya = pl.pallas_call(
        functools.partial(first_kernel, n_gx, n_gy),
        name="route_and_first_sweep",
        in_specs=[vmem] * 6 + [hbm] * 4,
        out_specs=[hbm] * 3 + [vmem] * 4,
        out_shape=[whole, whole, shape((planes, rows, cols), bf16)] + sides,
        scratch_shapes=[
            pltpu.VMEM((peers, SUB, HALF), f32),
            pltpu.VMEM((peers, SUB, HALF), f32),
            pltpu.VMEM((3, planes, rows, cols), bf16),
            pltpu.VMEM((planes, rows, cols), bf16),
            pltpu.VMEM((planes, rows, cols), bf16),
        ]
        + field_scratch(planes, rows, cols)
        + [
            pltpu.VMEM((peers * CAP, 3 * cols), bf16),
            pltpu.VMEM((peers * CAP, 3 * cols), bf16),
        ]
        + [pltpu.VMEM(e, f32) for e in edges]
        + [dma((5,)), dma((2 * planes // GROUP + 1,)), dma, dma, dma, dma((2, 4)), dma((2, 4))],
        compiler_params=pltpu.CompilerParams(
            collective_id=0, has_side_effects=True, vmem_limit_bytes=60 << 20
        ),
    )(
        window_source.reshape(flat),
        window_block.reshape(flat),
        window_count.reshape(flat),
        window_weight.reshape(flat),
        observed,
        interp_weight,
        velocity,
        kinetic_energy,
        dissipation_rate,
        adjoint_start,
    )
    starts = (0, 1, 2, 4, 8, 12)
    return pl.pallas_call(
        functools.partial(second_kernel, n_gx, n_gy, starts),
        name="second_sweep",
        in_specs=[hbm] * 4 + [vmem] * 4,
        out_specs=hbm,
        out_shape=whole,
        scratch_shapes=[pltpu.VMEM((3, planes, rows, cols), bf16)]
        + field_scratch(planes, rows, cols)
        + [dma((5, len(starts))), dma],
        compiler_params=pltpu.CompilerParams(vmem_limit_bytes=60 << 20),
    )(forcing, velocity, visc, adjoint, xh, yc, xa, ya)


def solution(mesh):
    placed = (
        P(None, None, "gx", "gy"),
        P(None, "gx", "gy"),
        P(None, "gx", "gy"),
        P(None, None, "gx", "gy"),
        P(),
        P(None, ("gx", "gy"), None),
        P(("gx", "gy")),
        P(("gx", "gy"), None),
        P(("gx", "gy")),
        P(("gx", "gy")),
    )
    return jax.shard_map(
        functools.partial(local, mesh.shape["gx"], mesh.shape["gy"]),
        mesh=mesh,
        in_specs=placed,
        out_specs=P(None, None, "gx", "gy"),
        check_vma=False,
    )
```

time: 69.4 us -> 57.1 us (0.82)
  Pallas kernels: 69.1 us -> 56.9 us
    pallas_call x1, Pallas kernels: 55.1 us -> 43.9 us  [local(): pl.pallas_call(functools.partial(first_kernel, n_gx, n_gy), name='route_a...]
    pallas_call x1, Pallas kernels: 14 us -> 13 us  [local(): pl.pallas_call(functools.partial(second_kernel, n_gx, n_gy, starts), name...]
where the time goes in v3:
time: 57.1 us; the launch traced here: 56.9 us
  Pallas kernels  56.9 us (100%)
    pallas_call x1, Pallas kernels, local(): pl.pallas_call(functools.partial(first_kernel, n_gx, n_gy), name='route_a...  43.9 us
    pallas_call x1, Pallas kernels, local(): pl.pallas_call(functools.partial(second_kernel, n_gx, n_gy, starts), name...  13 us

profile of v3, /device:TPU:1, one launch (start us, length us, event | category | flops | bytes accessed | tf_op | source)
XLA Modules:
  0.0 56.9 jit_solution(11717720000672962087)
XLA Ops:
  0.0 43.9 %route_and_first_sweep.1 = (f32[3,16,128,256]{3,2,1,0:T(8,128)}, f32[3,16,128,256]{3,2,1,0:T(8,128)}, bf16[16,128,256]{2,1,0:T(8,128)(2,1)}, f32[2,80,256]{2,1,0...) custom-call(s32[1,256]{1,0:T(1,128)} %bitcast.4, s32[1,256]{1,0:T(1,128)} %bitcast.5, ...), custom_call_target="tpu_custom_call" | custom-call | tf_op jit(solution)/shard_map/route_and_first_sweep/pallas_call | solution.py:555
  43.9 13.0 %second_sweep.1 = f32[3,16,128,256]{3,2,1,0:T(8,128)} custom-call(f32[3,16,128,256]{3,2,1,0:T(8,128)} %get-tuple-element.12.refs_0_, bf16[3,16,128,256]{3,2,1,0:T(8,128)(2,1)} %refs_1_.1, bf16[16,128,256]{2,1,0:T(8,128)(2,1)} %get-tuple-element.13.refs_2_, f32[3,16,128,256]{3,2,1,0:T(8,128)} %get-tuple-element.14.refs_3_, ...), custom_call_target="tpu_custom_call" | custom-call | tf_op jit(solution)/shard_map/second_sweep/pallas_call | solution.py:591

commit v4 on v3

--- a/solution.py
+++ b/solution.py
@@ -18,7 +18,7 @@
 half_step = 0.5 * pseudo_step
 
 HALF = 2 * LANES
-BLOCK, COUNT, WEIGHT = 0, 1, 2
+PLANE, ROW, COUNT, WEIGHT = 0, 1, 2, 3
 PAD = 8
 
 
@@ -35,41 +35,31 @@
     return out
 
 
-def fill_slots(source, block, count, weight, obs_ref, slots_ref):
+def fill_slots(source, block, count, weight, obs_ref, slots_ref, rows):
     windows = source.shape[1]
     peers = slots_ref.shape[0]
     slots = peers * CAP
     f32 = jnp.float32
-    meta = jnp.concatenate(
-        [
-            block.astype(f32),
-            count.astype(f32),
-            weight,
-            source.astype(f32),
-            jnp.zeros((LANES - 4, windows), f32),
-        ],
-        axis=0,
-    ).T
+    meta = [block // rows, block % rows, count] + split(weight, 3) + [source]
+    meta = [row.astype(f32) for row in meta]
+    meta = jnp.concatenate(meta + [jnp.zeros((LANES - len(meta), windows), f32)], axis=0).T
     first = lax.broadcasted_iota(jnp.int32, (windows, windows), 0)
     second = lax.broadcasted_iota(jnp.int32, (windows, windows), 1)
-    same = (meta[:, 3:4] == source.astype(f32)) & (first < second)
+    same = (meta[:, 6:7] == source.astype(f32)) & (first < second)
     place = jnp.sum(same.astype(f32), axis=0, keepdims=True).astype(jnp.int32)
     chosen = lax.broadcasted_iota(jnp.int32, (slots, windows), 0) == source * CAP + place
     chosen = chosen.astype(jnp.bfloat16)
     top = lax.broadcasted_iota(jnp.int32, (slots // SUB, SUB, LANES), 1) < CAP
     quarters = []
     for values in (obs_ref[0], obs_ref[1], obs_ref[2], meta):
-        total = jnp.zeros((slots, LANES), f32)
-        for piece in reversed(split(values, 3)):
-            total = total + jnp.dot(chosen, piece, preferred_element_type=f32)
+        total = jnp.dot(chosen, values.astype(jnp.bfloat16), preferred_element_type=f32)
         quarters.append(total.reshape(slots // SUB, SUB, LANES))
     for h in range(2):
         upper, lower = quarters[h], quarters[2 + h]
         even = jnp.where(top, upper, pltpu.roll(lower, CAP, axis=1))
         odd = jnp.where(top, pltpu.roll(upper, CAP, axis=1), lower)
-        slots_ref[:, :, h * LANES : (h + 1) * LANES] = jnp.stack([even, odd], axis=1).reshape(
-            peers, SUB, LANES
-        )
+        both = jnp.stack([even, odd], axis=1).reshape(peers, SUB, LANES)
+        slots_ref[:, :, h * LANES : (h + 1) * LANES] = both.astype(jnp.bfloat16)
 
 
 def read_slots(recv_ref):
@@ -77,7 +67,8 @@
     top = lax.broadcasted_iota(jnp.int32, (peers // 2, SUB, LANES), 1) < CAP
     quarters = [None] * 4
     for h in range(2):
-        pairs = recv_ref[:, :, h * LANES : (h + 1) * LANES].reshape(peers // 2, 2, SUB, LANES)
+        half = recv_ref[:, :, h * LANES : (h + 1) * LANES].astype(jnp.float32)
+        pairs = half.reshape(peers // 2, 2, SUB, LANES)
         even, odd = pairs[:, 0], pairs[:, 1]
         upper = jnp.where(top, even, pltpu.roll(odd, CAP, axis=1))
         lower = jnp.where(top, pltpu.roll(even, CAP, axis=1), odd)
@@ -91,9 +82,9 @@
     slots = meta.shape[0]
     planes, rows, cols = vel_ref.shape[1:]
     weights = weight_ref[...]
-    block = meta[:, BLOCK : BLOCK + 1].astype(jnp.int32)
+    block = (meta[:, PLANE : PLANE + 1] * rows + meta[:, ROW : ROW + 1]).astype(jnp.int32)
     count = meta[:, COUNT : COUNT + 1].astype(jnp.int32)
-    scale = meta[:, WEIGHT : WEIGHT + 1]
+    scale = sum(meta[:, WEIGHT + k : WEIGHT + k + 1] for k in (2, 1, 0))
     inside = lax.broadcasted_iota(jnp.int32, (slots, cols), 1) < count
     group = 4
     lines = [jnp.zeros((slots, cols), jnp.float32) for _ in range(3)]
@@ -134,7 +125,7 @@
             at = slice(c * planes, (c + 1) * planes)
             xe[side, at, :] = xe[side, at, :] + total[side * planes : (side + 1) * planes, c * cols : (c + 1) * cols]
     lanes = lane_iota(slots)
-    plane = meta[:, BLOCK : BLOCK + 1].astype(jnp.int32) // rows
+    plane = meta[:, PLANE : PLANE + 1].astype(jnp.int32)
     values = jnp.zeros((slots, LANES), f32)
     for c in range(3):
         for side in range(2):
@@ -188,11 +179,16 @@
         ye[at, :] = packed
 
 
-def from_sides(yh, index):
+def scaled_from(shape, axis, first, factor):
+    return jnp.where(lax.broadcasted_iota(jnp.int32, shape, axis) < first, 1.0, factor)
+
+
+def from_sides(below, above, index):
     inner = inside_flags(*index)
-    below = pltpu.roll(yh[0], 1, axis=1) * inner[2]
-    above = pltpu.roll(yh[1], LANES - 1, axis=1) * inner[3]
-    return jnp.where(lane_iota(below.shape[0]) % 2 == 1, below, above)
+    odd = lane_iota(below.shape[0]) % 2 == 1
+    below, above = below * inner[2], above * inner[3]
+    moved = jnp.where(odd, pltpu.roll(below, 1, axis=1), pltpu.roll(above, LANES - 1, axis=1))
+    return moved, jnp.where(odd, below, above)
 
 
 def inside_flags(n_gx, n_gy):
@@ -227,19 +223,67 @@
         ux[z + 1, h, PAD : PAD + rows, :] = vel[0, z, :, half].astype(jnp.float32) * half_step
 
 
-def set_rows(planes, rows, index, xa, xh, adj, ux, vv):
-    inner = inside_flags(*index)
+def clear_rows(planes, rows, adj, ux, vv):
+    zero = jnp.zeros((PAD, LANES), jnp.float32)
+    for at in (0, PAD + rows):
+        for z in range(planes):
+            for h in range(2):
+                for ref in (ux, vv):
+                    ref[z + 1, h, at : at + PAD, :] = zero
+                for c in range(3):
+                    adj[c, z + 1, h, at : at + PAD, :] = zero
+
+
+def add_rows(planes, rows, xe, xh, out):
+    for side, at, sign in ((0, 0, 1.0), (1, rows - 1, -1.0)):
+        v_out = xh[side, 4 * planes : 5 * planes, :]
+        coef = xe[side, 4 * planes : 5 * planes, :] + v_out + sign * xh[side, 3 * planes : 4 * planes, :]
+        for c in range(3):
+            mine = slice(c * planes, (c + 1) * planes)
+            share = coef * xh[side, mine, :] - v_out * xe[side, mine, :]
+            for z in range(planes):
+                out[c, z, at : at + 1, :] = out[c, z, at : at + 1, :] + share[z : z + 1, :]
+
+
+def column_fix(planes, own, outside, normal):
+    lanes = lane_iota(own.shape[0])
+    coef = own + outside + jnp.where(lanes % 2 == 1, normal, -normal)
+
+    def spread(x):
+        for_c = [pltpu.roll(x, LANES - 2 * planes * (3 - c), axis=1) for c in range(3)]
+        return jnp.where(lanes < 2 * planes, for_c[0], jnp.where(lanes < 4 * planes, for_c[1], for_c[2]))
+
+    share = spread(coef) * outside - spread(outside) * own
+    return jnp.where(lanes < 6 * planes, share, 0.0)
+
+
+def add_columns(planes, rows, fix, out):
+    lanes = lane_iota()
+
+    @pl.loop(0, rows // SUB)
+    def _(r):
+        at = pl.ds(pl.multiple_of(r * SUB, SUB), SUB)
+        packed = fix[at, :]
+        for k in range(3 * planes):
+            c, z = k // planes, k % planes
+            moved = pltpu.roll(packed, LANES - 1 - 2 * k, axis=1)
+            left, right = slice(0, LANES), slice(LANES, 2 * LANES)
+            out[c, z, at, left] = out[c, z, at, left] + jnp.where(lanes == 0, moved, 0.0)
+            out[c, z, at, right] = out[c, z, at, right] + jnp.where(lanes == LANES - 1, moved, 0.0)
+
+
+def set_rows(planes, rows, xa, xh, adj, ux, vv):
     for side, at in ((0, PAD - 1), (1, PAD + rows)):
         for z in range(planes):
             for h in range(2):
                 half = slice(h * LANES, (h + 1) * LANES)
                 for c in range(3):
                     k = c * planes + z
-                    adj[c, z + 1, h, at : at + 1, :] = xa[side, k : k + 1, half] * inner[side]
+                    adj[c, z + 1, h, at : at + 1, :] = xa[side, k : k + 1, half]
                 k = 3 * planes + z
-                ux[z + 1, h, at : at + 1, :] = xh[side, k : k + 1, half] * inner[side]
+                ux[z + 1, h, at : at + 1, :] = xh[side, k : k + 1, half]
                 k = 4 * planes + z
-                vv[z + 1, h, at : at + 1, :] = xh[side, k : k + 1, half] * inner[side]
+                vv[z + 1, h, at : at + 1, :] = xh[side, k : k + 1, half]
 
 
 def up_down(pair, outer, first, last):
@@ -298,9 +342,10 @@
 
 
 def first_kernel(n_gx, n_gy, *refs):
-    (source, block, count, weight, obs, weights, vel_in, ke_in, dr_in, adj_in,
-     out_hbm, f_hbm, visc_hbm, xh, yc, xa, ya,
-     slots, recv, vel, ke, dr, visc, adj, ux, uy, uz, vv, yhs, out, frc, high, low, xe, ye, yh, xe2, ye2,
+    (source, block, count, weight, obs_in, weights_in, vel_in, ke_in, dr_in, adj_in,
+     out_hbm, f_hbm, visc_hbm, xh_hbm, yc_hbm, xa, ya,
+     slots, recv, obs, weights, vel, ke, dr, visc, adj, ux, uy, uz, vv, yhs, out, frc, high, low, xe, xh, ye, xe2, ye2, yfix,
+     x_out, x_in, y_out, y_in, x_out2, y_out2,
      load, save, all_send, all_recv, local_sem, send, received) = refs
     planes, rows, cols = visc.shape
     peers = n_gx * n_gy
@@ -320,8 +365,8 @@
         sides = (
             (x_from.at[1], x_to.at[0], upper_x),
             (x_from.at[0], x_to.at[1], lower_x),
-            (y_from, y_to.at[0], upper_y),
-            (y_from, y_to.at[1], lower_y),
+            (y_from[1], y_to.at[0], upper_y),
+            (y_from[0], y_to.at[1], lower_y),
         )
         return [
             pltpu.make_async_remote_copy(
@@ -342,7 +387,11 @@
         )
         for h in range(2)
     ]
-    for copy in loads:
+    ahead = [
+        pltpu.make_async_copy(obs_in, obs, load.at[5]),
+        pltpu.make_async_copy(weights_in, weights, load.at[6]),
+    ]
+    for copy in ahead + loads:
         copy.start()
     barrier = pltpu.get_barrier_semaphore()
 
@@ -350,7 +399,9 @@
     def _(step):
         pl.semaphore_signal(barrier, inc=1, device_id=device(step)[1], device_id_type=MESH)
 
-    fill_slots(source[...], block[...], count[...], weight[...], obs, slots)
+    for copy in ahead:
+        copy.wait()
+    fill_slots(source[...], block[...], count[...], weight[...], obs, slots, rows)
     clear_outside(planes, rows, cols, adj, uz, vv)
     for copy in loads[:3]:
         copy.wait()
@@ -381,32 +432,57 @@
     pack_columns(list(enumerate(starts + visc_fields)), rows, ye.at[0])
     pack_columns([(3 * planes + z, of_uy(z)) for z in range(planes)], rows, ye.at[1])
 
+    bf16, f32 = jnp.bfloat16, jnp.float32
+    unscale_rows = scaled_from(xe.shape[1:], 0, 3 * planes, 1.0 / half_step)
+    unscale_lanes = scaled_from((rows, LANES), 1, 6 * planes, 1.0 / half_step)
+    for side in range(2):
+        x_out[side] = (xe[side] * unscale_rows).astype(bf16)
+    odd = lane_iota(rows) % 2 == 1
+    main, normal = ye[0] * unscale_lanes, ye[1] * unscale_lanes
+    y_out[0] = jnp.where(odd, main, pltpu.roll(normal, LANES - 1, axis=1)).astype(bf16)
+    y_out[1] = jnp.where(odd, pltpu.roll(normal, 1, axis=1), main).astype(bf16)
+
     pl.semaphore_wait(barrier, peers - 1)
-    copies = edge_copies(0, xe, ye, xh, yh)
+    copies = edge_copies(0, x_out, (y_out.at[0], y_out.at[1]), x_in, y_in)
     for copy in copies:
         copy.start()
     own = pltpu.make_async_copy(slots.at[me], recv.at[me], local_sem)
     own.start()
 
-    @pl.loop(1, peers)
-    def _(step):
+    def send_slots(step):
         peer, where = device(step)
         pltpu.make_async_remote_copy(
             slots.at[peer], recv.at[me], all_send, all_recv, device_id=where, device_id_type=MESH
         ).start()
 
+    pl.loop(1, peers)(send_slots)
+
+    clear_rows(planes, rows, adj, ux, vv)
+    yhs[...] = jnp.zeros_like(yhs)
+
+    @pl.loop(0, planes)
+    def _(z):
+        sweep_plane(z, planes, rows, adj, ux, uy, uz, vv, yhs, None, out)
+
     for copy in copies:
         copy.wait()
     index = (n_gx, n_gy)
-    set_rows(planes, rows, index, xh, xh, adj, ux, vv)
-    for k in range(2):
-        sides = from_sides(yh.at[:, k], index)
-        yc[k] = sides
-        yhs[k] = sides
-
-    @pl.loop(0, planes)
-    def _(z):
-        sweep_plane(z, planes, rows, adj, ux, uy, uz, vv, yhs, None, out)
+    inner = inside_flags(*index)
+    scale_rows = scaled_from(xe.shape[1:], 0, 3 * planes, half_step)
+    scale_lanes = scaled_from((rows, LANES), 1, 6 * planes, half_step)
+    for side in range(2):
+        xh[side] = x_in[side].astype(f32) * (scale_rows * inner[side])
+    below, above = (y_in[side].astype(f32) * scale_lanes for side in range(2))
+    yhs[0], yhs[1] = from_sides(below, above, index)
+    side_saves = [
+        pltpu.make_async_copy(xh, xh_hbm, save.at[9]),
+        pltpu.make_async_copy(yhs, yc_hbm, save.at[10]),
+    ]
+    for copy in side_saves:
+        copy.start()
+    add_rows(planes, rows, xe, xh, out)
+    fix = column_fix(planes, ye[0], yhs[0], yhs[1])
+    yfix[...] = fix
 
     def of_out(c, z):
         return lambda at, h: out[c, z, at, slice(h * LANES, (h + 1) * LANES)]
@@ -414,6 +490,14 @@
     news = [of_out(c, z) for c in range(3) for z in range(planes)]
     pack_rows(news, rows, cols, xe2)
     pack_columns(list(enumerate(news)), rows, ye2)
+    ye2[...] = ye2[...] + fix
+    for side, at in ((0, 0), (1, rows - 1)):
+        row = jnp.broadcast_to(fix[at : at + 1], (3 * planes, LANES))
+        spot = lax.broadcasted_iota(jnp.int32, row.shape, 1)
+        field = 2 * lax.broadcasted_iota(jnp.int32, row.shape, 0)
+        for which, lane, half in ((1, 0, slice(0, LANES)), (0, LANES - 1, slice(LANES, 2 * LANES))):
+            corner = jnp.sum(jnp.where(spot == field + which, row, 0.0), axis=1, keepdims=True)
+            xe2[side, :, half] = xe2[side, :, half] + jnp.where(spot == lane, corner, 0.0)
 
     own.wait()
     rest = pl.ds(0, peers - 1)
@@ -421,11 +505,15 @@
     pltpu.make_async_copy(recv.at[rest], recv.at[rest], all_recv).wait()
     quarters = read_slots(recv)
     edge_values = line_forcing(quarters, vel, weights, high, low)
-    block = quarters[3].T[BLOCK : BLOCK + 1].astype(jnp.int32)
+    across = quarters[3].T
+    block = (across[PLANE : PLANE + 1] * rows + across[ROW : ROW + 1]).astype(jnp.int32)
     force_edges(block, quarters[3], edge_values, high, low, planes, rows, xe2, ye2)
-    copies = edge_copies(1, xe2, ye2, xa, ya)
+    x_out2[...] = xe2[...].astype(bf16)
+    y_out2[...] = ye2[...].astype(bf16)
+    copies = edge_copies(1, x_out2, (y_out2, y_out2), xa, ya)
     for copy in copies:
         copy.start()
+    add_columns(planes, rows, yfix, out)
     saves = []
     for q in range(planes // GROUP):
         place_lines(q, block, high, low, frc, out)
@@ -434,15 +522,15 @@
         saves.append(pltpu.make_async_copy(out.at[:, at], out_hbm.at[:, at], save.at[2 * q + 1]))
         for copy in saves[-2:]:
             copy.start()
-    for copy in copies + saves:
+    for copy in copies + saves + side_saves:
         copy.wait()
     visc_save.wait()
 
 
 def second_kernel(n_gx, n_gy, starts, *refs):
-    (f_in, vel_in, visc_in, adj_in, xh, yc, xa, ya,
+    (f_in, vel_in, visc_in, adj_in, xh_in, yc_in, xa_in, ya_in,
      out_hbm,
-     vel, visc, adj, ux, uy, uz, vv, yhs, out, frc, load, save) = refs
+     vel, visc, adj, ux, uy, uz, vv, yhs, out, frc, xh, yc, x_in, y_in, xa, load, save) = refs
     planes, rows, cols = visc.shape
     ends = starts[1:] + (planes,)
 
@@ -463,14 +551,24 @@
         ]
 
     groups = [group(g) for g in range(len(starts))]
-    for copies in groups:
+    sides = [
+        pltpu.make_async_copy(a, b, load.at[5, k])
+        for k, (a, b) in enumerate(((xh_in, xh), (xa_in, x_in), (yc_in, yc), (ya_in, y_in)))
+    ]
+    for copies in [sides] + groups:
         for copy in copies:
             copy.start()
     clear_outside(planes, rows, cols, adj, uz, vv)
+    for copy in sides:
+        copy.wait()
     index = (n_gx, n_gy)
-    set_rows(planes, rows, index, xa, xh, adj, ux, vv)
+    inner = inside_flags(*index)
+    for side in range(2):
+        xa[side] = x_in[side].astype(jnp.float32) * inner[side]
+    set_rows(planes, rows, xa, xh, adj, ux, vv)
+    below, above = (y_in[side].astype(jnp.float32) for side in range(2))
     adjoint_lanes = lane_iota(rows) < 6 * planes
-    yhs[0] = jnp.where(adjoint_lanes, from_sides(ya, index), yc[0])
+    yhs[0] = jnp.where(adjoint_lanes, from_sides(below, above, index)[0], yc[0])
     yhs[1] = yc[1]
 
     def fields(z):
@@ -541,13 +639,22 @@
     sides = [
         shape((2, 5 * planes, cols), f32),
         shape((2, rows, LANES), f32),
-        shape((2, 3 * planes, cols), f32),
-        shape((2, rows, LANES), f32),
+        shape((2, 3 * planes, cols), bf16),
+        shape((2, rows, LANES), bf16),
     ]
     edges = [
         (2, 5 * planes, cols),
+        (2, 5 * planes, cols),
         (2, rows, LANES),
-        (2, 2, rows, LANES),
+        (2, 3 * planes, cols),
+        (rows, LANES),
+        (rows, LANES),
+    ]
+    messages = [
+        (2, 5 * planes, cols),
+        (2, 5 * planes, cols),
+        (2, rows, LANES),
+        (2, rows, LANES),
         (2, 3 * planes, cols),
         (rows, LANES),
     ]
@@ -555,12 +662,14 @@
     adjoint, forcing, visc, xh, yc, xa, ya = pl.pallas_call(
         functools.partial(first_kernel, n_gx, n_gy),
         name="route_and_first_sweep",
-        in_specs=[vmem] * 6 + [hbm] * 4,
-        out_specs=[hbm] * 3 + [vmem] * 4,
+        in_specs=[vmem] * 4 + [hbm] * 6,
+        out_specs=[hbm] * 7,
         out_shape=[whole, whole, shape((planes, rows, cols), bf16)] + sides,
         scratch_shapes=[
-            pltpu.VMEM((peers, SUB, HALF), f32),
-            pltpu.VMEM((peers, SUB, HALF), f32),
+            pltpu.VMEM((peers, SUB, HALF), bf16),
+            pltpu.VMEM((peers, SUB, HALF), bf16),
+            pltpu.VMEM(observed.shape, f32),
+            pltpu.VMEM(interp_weight.shape, bf16),
             pltpu.VMEM((3, planes, rows, cols), bf16),
             pltpu.VMEM((planes, rows, cols), bf16),
             pltpu.VMEM((planes, rows, cols), bf16),
@@ -570,8 +679,8 @@
             pltpu.VMEM((peers * CAP, 3 * cols), bf16),
             pltpu.VMEM((peers * CAP, 3 * cols), bf16),
         ]
-        + [pltpu.VMEM(e, f32) for e in edges]
-        + [dma((5,)), dma((2 * planes // GROUP + 1,)), dma, dma, dma, dma((2, 4)), dma((2, 4))],
+        + [pltpu.VMEM(e, f32) for e in edges] + [pltpu.VMEM(e, bf16) for e in messages]
+        + [dma((7,)), dma((2 * planes // GROUP + 3,)), dma, dma, dma, dma((2, 4)), dma((2, 4))],
         compiler_params=pltpu.CompilerParams(
             collective_id=0, has_side_effects=True, vmem_limit_bytes=60 << 20
         ),
@@ -591,12 +700,14 @@
     return pl.pallas_call(
         functools.partial(second_kernel, n_gx, n_gy, starts),
         name="second_sweep",
-        in_specs=[hbm] * 4 + [vmem] * 4,
+        in_specs=[hbm] * 8,
         out_specs=hbm,
         out_shape=whole,
         scratch_shapes=[pltpu.VMEM((3, planes, rows, cols), bf16)]
         + field_scratch(planes, rows, cols)
-        + [dma((5, len(starts))), dma],
+        + [pltpu.VMEM(side.shape, side.dtype) for side in sides]
+        + [pltpu.VMEM(sides[2].shape, f32)]
+        + [dma((6, len(starts))), dma],
         compiler_params=pltpu.CompilerParams(vmem_limit_bytes=60 << 20),
     )(forcing, velocity, visc, adjoint, xh, yc, xa, ya)
 

time: 57.1 us -> 49 us (0.86)
  Pallas kernels: 56.9 us -> 48.8 us
    pallas_call x1, Pallas kernels: 43.9 us -> 36.7 us  [local(): pl.pallas_call(functools.partial(first_kernel, n_gx, n_gy), name='route_a...]
    pallas_call x1, Pallas kernels: 13 us -> 12.1 us  [local(): pl.pallas_call(functools.partial(second_kernel, n_gx, n_gy, starts), name...]
where the time goes in v4:
time: 49 us; the launch traced here: 48.8 us
  Pallas kernels  48.8 us (100%)
    pallas_call x1, Pallas kernels, local(): pl.pallas_call(functools.partial(first_kernel, n_gx, n_gy), name='route_a...  36.7 us
    pallas_call x1, Pallas kernels, local(): pl.pallas_call(functools.partial(second_kernel, n_gx, n_gy, starts), name...  12.1 us

profile of v4, /device:TPU:1, one launch (start us, length us, event | category | flops | bytes accessed | tf_op | source)
XLA Modules:
  0.0 48.8 jit_solution(2683227032408114359)
XLA Ops:
  0.0 36.7 %route_and_first_sweep.1 = (f32[3,16,128,256]{3,2,1,0:T(8,128)}, f32[3,16,128,256]{3,2,1,0:T(8,128)}, bf16[16,128,256]{2,1,0:T(8,128)(2,1)}, f32[2,80,256]{2,1,0...) custom-call(s32[1,256]{1,0:T(1,128)} %bitcast.4, s32[1,256]{1,0:T(1,128)} %bitcast.5, ...), custom_call_target="tpu_custom_call" | custom-call | tf_op jit(solution)/shard_map/route_and_first_sweep/pallas_call | solution.py:662
  36.7 12.1 %second_sweep.1 = f32[3,16,128,256]{3,2,1,0:T(8,128)} custom-call(f32[3,16,128,256]{3,2,1,0:T(8,128)} %get-tuple-element.12.refs_0_, bf16[3,16,128,256]{3,2,1,0:T(8,128)(2,1)} %refs_1_.1, bf16[16,128,256]{2,1,0:T(8,128)(2,1)} %get-tuple-element.13.refs_2_, f32[3,16,128,256]{3,2,1,0:T(8,128)} %get-tuple-element.14.refs_3_, ...), custom_call_target="tpu_custom_call" | custom-call | tf_op jit(solution)/shard_map/second_sweep/pallas_call | solution.py:700

commit v5 on v4

--- a/solution.py
+++ b/solution.py
@@ -215,7 +215,8 @@
 
 def set_fields(z, vel, visc, ux, uy, uz, vv):
     rows = visc.shape[1]
-    uy[z + 1] = vel[1, z].astype(jnp.float32) * half_step
+    if uy is not None:
+        uy[z + 1] = vel[1, z].astype(jnp.float32) * half_step
     uz[z + 1] = vel[2, z].astype(jnp.float32) * half_step
     for h in range(2):
         half = slice(h * LANES, (h + 1) * LANES)
@@ -257,19 +258,17 @@
     return jnp.where(lanes < 6 * planes, share, 0.0)
 
 
-def add_columns(planes, rows, fix, out):
+def add_columns(q, planes, rows, fix, out):
     lanes = lane_iota()
-
-    @pl.loop(0, rows // SUB)
-    def _(r):
-        at = pl.ds(pl.multiple_of(r * SUB, SUB), SUB)
+    left, right = slice(0, LANES), slice(LANES, 2 * LANES)
+    for r in range(rows // SUB):
+        at = slice(r * SUB, (r + 1) * SUB)
         packed = fix[at, :]
-        for k in range(3 * planes):
-            c, z = k // planes, k % planes
-            moved = pltpu.roll(packed, LANES - 1 - 2 * k, axis=1)
-            left, right = slice(0, LANES), slice(LANES, 2 * LANES)
-            out[c, z, at, left] = out[c, z, at, left] + jnp.where(lanes == 0, moved, 0.0)
-            out[c, z, at, right] = out[c, z, at, right] + jnp.where(lanes == LANES - 1, moved, 0.0)
+        for c in range(3):
+            for z in range(q * GROUP, (q + 1) * GROUP):
+                moved = pltpu.roll(packed, LANES - 1 - 2 * (c * planes + z), axis=1)
+                out[c, z, at, left] = out[c, z, at, left] + jnp.where(lanes == 0, moved, 0.0)
+                out[c, z, at, right] = out[c, z, at, right] + jnp.where(lanes == LANES - 1, moved, 0.0)
 
 
 def set_rows(planes, rows, xa, xh, adj, ux, vv):
@@ -295,23 +294,42 @@
     return up, down
 
 
-def sweep_plane(z, planes, rows, adj, ux, uy, uz, vv, yhs, forcing, out):
+def sweep_plane(z, planes, rows, adj, ux, uz, vv, vel, visc, yhs, forcing, out):
     lanes = lane_iota()
     first, last = lanes == 0, lanes == LANES - 1
     here = z + 1
     both = (slice(0, LANES), slice(LANES, 2 * LANES))
+    zero = jnp.zeros((SUB, LANES), jnp.float32)
+
+    def outer(edges, k):
+        return zero if edges is None else pltpu.roll(edges, LANES - 1 - 2 * (k * planes + z), axis=1)
+
+    def turned(ref, index, pair_rows):
+        out = []
+        for half in both:
+            x = ref[(*index, pair_rows, half)]
+            up, down = pltpu.roll(x, LANES - 1, axis=1), pltpu.roll(x, 1, axis=1)
+            out.append([y.astype(jnp.float32) * half_step for y in (up, down)])
+        return out
+
+    def joined(field, strip, outside):
+        (left_up, left_down), (right_up, right_down) = (
+            [y[strip * SUB : (strip + 1) * SUB] for y in half] for half in field
+        )
+        up = (jnp.where(last, right_up, left_up), jnp.where(last, outside, right_up))
+        down = (jnp.where(first, outside, left_down), jnp.where(first, left_down, right_down))
+        return up, down
 
     for r in range(rows // SUB):
         at = slice(r * SUB, (r + 1) * SUB)
         mid, plus, minus = (slice(at.start + PAD + d, at.stop + PAD + d) for d in (0, 1, -1))
-        edges = [yhs[0, at, :], yhs[1, at, :]]
-
-        def outer(which, k):
-            return pltpu.roll(edges[which], LANES - 1 - 2 * (k * planes + z), axis=1)
-
+        edges = (None, None) if yhs is None else (yhs[0, at, :], yhs[1, at, :])
+        if r % 2 == 0:
+            pair_rows = slice(r * SUB, (r + 2) * SUB)
+            v_turned, u_turned = turned(visc, (z,), pair_rows), turned(vel, (1, z), pair_rows)
         v = [vv[here, h, mid, :] for h in range(2)]
-        v_yp, v_ym = up_down(v, outer(0, 3), first, last)
-        u_yp, u_ym = up_down([uy[here, at, half] for half in both], outer(1, 3), first, last)
+        v_yp, v_ym = joined(v_turned, r % 2, outer(edges[0], 3))
+        u_yp, u_ym = joined(u_turned, r % 2, outer(edges[1], 3))
         coef = []
         for h in range(2):
             n_xp, n_xm = v[h] + vv[here, h, plus, :], v[h] + vv[here, h, minus, :]
@@ -330,7 +348,7 @@
             )
         for c in range(3):
             a = [adj[c, here, h, mid, :] for h in range(2)]
-            a_yp, a_ym = up_down(a, outer(0, c), first, last)
+            a_yp, a_ym = up_down(a, outer(edges[0], c), first, last)
             for h in range(2):
                 k = coef[h]
                 value = k[0] * a[h] + (k[1] * adj[c, here, h, plus, :] + k[2] * adj[c, here, h, minus, :])
@@ -458,11 +476,10 @@
     pl.loop(1, peers)(send_slots)
 
     clear_rows(planes, rows, adj, ux, vv)
-    yhs[...] = jnp.zeros_like(yhs)
 
     @pl.loop(0, planes)
     def _(z):
-        sweep_plane(z, planes, rows, adj, ux, uy, uz, vv, yhs, None, out)
+        sweep_plane(z, planes, rows, adj, ux, uz, vv, vel, visc, None, None, out)
 
     for copy in copies:
         copy.wait()
@@ -513,9 +530,9 @@
     copies = edge_copies(1, x_out2, (y_out2, y_out2), xa, ya)
     for copy in copies:
         copy.start()
-    add_columns(planes, rows, yfix, out)
     saves = []
     for q in range(planes // GROUP):
+        add_columns(q, planes, rows, yfix, out)
         place_lines(q, block, high, low, frc, out)
         at = pl.ds(q * GROUP, GROUP)
         saves.append(pltpu.make_async_copy(frc.at[:, at], f_hbm.at[:, at], save.at[2 * q]))
@@ -572,7 +589,7 @@
     yhs[1] = yc[1]
 
     def fields(z):
-        set_fields(z, vel, visc, ux, uy, uz, vv)
+        set_fields(z, vel, visc, ux, None, uz, vv)
 
     for copy in groups[0]:
         copy.wait()
@@ -591,7 +608,7 @@
         def _():
             fields(z + 1)
 
-        sweep_plane(z, planes, rows, adj, ux, uy, uz, vv, yhs, frc, out)
+        sweep_plane(z, planes, rows, adj, ux, uz, vv, vel, visc, yhs, frc, out)
         pltpu.make_async_copy(out.at[:, z], out_hbm.at[:, z], save).start()
 
     pltpu.make_async_copy(out, out_hbm, save).wait()

time: 49 us -> 45.3 us (0.924)
  Pallas kernels: 48.8 us -> 45.1 us
    pallas_call x1, Pallas kernels: 36.7 us -> 34 us  [local(): pl.pallas_call(functools.partial(first_kernel, n_gx, n_gy), name='route_a...]
    pallas_call x1, Pallas kernels: 12.1 us -> 11.1 us  [local(): pl.pallas_call(functools.partial(second_kernel, n_gx, n_gy, starts), name...]
where the time goes in v5:
time: 45.3 us; the launch traced here: 45.2 us
  Pallas kernels  45.1 us (100%)
    pallas_call x1, Pallas kernels, local(): pl.pallas_call(functools.partial(first_kernel, n_gx, n_gy), name='route_a...  34 us
    pallas_call x1, Pallas kernels, local(): pl.pallas_call(functools.partial(second_kernel, n_gx, n_gy, starts), name...  11.1 us

profile of v5, /device:TPU:1, one launch (start us, length us, event | category | flops | bytes accessed | tf_op | source)
XLA Modules:
  0.0 45.2 jit_solution(5106117175343442839)
XLA Ops:
  0.0 34.0 %route_and_first_sweep.1 = (f32[3,16,128,256]{3,2,1,0:T(8,128)}, f32[3,16,128,256]{3,2,1,0:T(8,128)}, bf16[16,128,256]{2,1,0:T(8,128)(2,1)}, f32[2,80,256]{2,1,0...) custom-call(s32[1,256]{1,0:T(1,128)} %bitcast.4, s32[1,256]{1,0:T(1,128)} %bitcast.5, ...), custom_call_target="tpu_custom_call" | custom-call | tf_op jit(solution)/shard_map/route_and_first_sweep/pallas_call | solution.py:679
  34.0 11.1 %second_sweep.1 = f32[3,16,128,256]{3,2,1,0:T(8,128)} custom-call(f32[3,16,128,256]{3,2,1,0:T(8,128)} %get-tuple-element.12.refs_0_, bf16[3,16,128,256]{3,2,1,0:T(8,128)(2,1)} %refs_1_.1, bf16[16,128,256]{2,1,0:T(8,128)(2,1)} %get-tuple-element.13.refs_2_, f32[3,16,128,256]{3,2,1,0:T(8,128)} %get-tuple-element.14.refs_3_, ...), custom_call_target="tpu_custom_call" | custom-call | tf_op jit(solution)/shard_map/second_sweep/pallas_call | solution.py:717

commit v6 on v5

--- a/solution.py
+++ b/solution.py
@@ -165,18 +165,21 @@
             xe[1, k : k + 1, half] = read(slice(rows - 1, rows), h)
 
 
-def pack_columns(fields, rows, ye):
+def pack_columns(jobs, rows):
     lanes = lane_iota()
-
-    @pl.loop(0, rows // SUB)
+    strips = 4
+
+    @pl.loop(0, rows // SUB // strips)
     def _(r):
-        at = pl.ds(pl.multiple_of(r * SUB, SUB), SUB)
-        packed = jnp.zeros((SUB, LANES), jnp.float32)
-        for k, read in fields:
-            ends = jnp.where(lanes == 0, read(at, 0), read(at, 1))
-            ends = pltpu.roll(ends, (2 * k + 1) % LANES, axis=1)
-            packed = jnp.where(lanes // 2 == k, ends, packed)
-        ye[at, :] = packed
+        for i in range(strips):
+            at = pl.ds(pl.multiple_of((r * strips + i) * SUB, SUB), SUB)
+            for fields, ye in jobs:
+                packed = jnp.zeros((SUB, LANES), jnp.float32)
+                for k, read in fields:
+                    ends = jnp.where(lanes == 0, read(at, 0), read(at, 1))
+                    ends = pltpu.roll(ends, (2 * k + 1) % LANES, axis=1)
+                    packed = jnp.where(lanes // 2 == k, ends, packed)
+                ye[at, :] = packed
 
 
 def scaled_from(shape, axis, first, factor):
@@ -447,8 +450,8 @@
     starts = [of_adj(c, z) for c in range(3) for z in range(planes)]
     visc_fields = [of_tall(vv, z) for z in range(planes)]
     pack_rows(starts + [of_tall(ux, z) for z in range(planes)] + visc_fields, rows, cols, xe)
-    pack_columns(list(enumerate(starts + visc_fields)), rows, ye.at[0])
-    pack_columns([(3 * planes + z, of_uy(z)) for z in range(planes)], rows, ye.at[1])
+    normals = [(3 * planes + z, of_uy(z)) for z in range(planes)]
+    pack_columns([(list(enumerate(starts + visc_fields)), ye.at[0]), (normals, ye.at[1])], rows)
 
     bf16, f32 = jnp.bfloat16, jnp.float32
     unscale_rows = scaled_from(xe.shape[1:], 0, 3 * planes, 1.0 / half_step)
@@ -506,7 +509,7 @@
 
     news = [of_out(c, z) for c in range(3) for z in range(planes)]
     pack_rows(news, rows, cols, xe2)
-    pack_columns(list(enumerate(news)), rows, ye2)
+    pack_columns([(list(enumerate(news)), ye2)], rows)
     ye2[...] = ye2[...] + fix
     for side, at in ((0, 0), (1, rows - 1)):
         row = jnp.broadcast_to(fix[at : at + 1], (3 * planes, LANES))
@@ -604,10 +607,7 @@
                 for copy in groups[g]:
                     copy.wait()
 
-        @pl.when(z + 1 < planes)
-        def _():
-            fields(z + 1)
-
+        fields(jnp.minimum(z + 1, planes - 1))
         sweep_plane(z, planes, rows, adj, ux, uz, vv, vel, visc, yhs, frc, out)
         pltpu.make_async_copy(out.at[:, z], out_hbm.at[:, z], save).start()
 

time: 45.3 us -> 43.4 us (0.958)
  Pallas kernels: 45.1 us -> 43.2 us
    pallas_call x1, Pallas kernels: 34 us -> 32.5 us  [local(): pl.pallas_call(functools.partial(first_kernel, n_gx, n_gy), name='route_a...]
where the time goes in v6:
time: 43.4 us; the launch traced here: 43.2 us
  Pallas kernels  43.2 us (100%)
    pallas_call x1, Pallas kernels, local(): pl.pallas_call(functools.partial(first_kernel, n_gx, n_gy), name='route_a...  32.5 us
    pallas_call x1, Pallas kernels, local(): pl.pallas_call(functools.partial(second_kernel, n_gx, n_gy, starts), name...  10.8 us

profile of v6, /device:TPU:1, one launch (start us, length us, event | category | flops | bytes accessed | tf_op | source)
XLA Modules:
  0.0 43.2 jit_solution(15191278237104738882)
XLA Ops:
  0.0 32.5 %route_and_first_sweep.1 = (f32[3,16,128,256]{3,2,1,0:T(8,128)}, f32[3,16,128,256]{3,2,1,0:T(8,128)}, bf16[16,128,256]{2,1,0:T(8,128)(2,1)}, f32[2,80,256]{2,1,0...) custom-call(s32[1,256]{1,0:T(1,128)} %bitcast.4, s32[1,256]{1,0:T(1,128)} %bitcast.5, ...), custom_call_target="tpu_custom_call" | custom-call | tf_op jit(solution)/shard_map/route_and_first_sweep/pallas_call | solution.py:679
  32.5 10.8 %second_sweep.1 = f32[3,16,128,256]{3,2,1,0:T(8,128)} custom-call(f32[3,16,128,256]{3,2,1,0:T(8,128)} %get-tuple-element.12.refs_0_, bf16[3,16,128,256]{3,2,1,0:T(8,128)(2,1)} %refs_1_.1, bf16[16,128,256]{2,1,0:T(8,128)(2,1)} %get-tuple-element.13.refs_2_, f32[3,16,128,256]{3,2,1,0:T(8,128)} %get-tuple-element.14.refs_3_, ...), custom_call_target="tpu_custom_call" | custom-call | tf_op jit(solution)/shard_map/second_sweep/pallas_call | solution.py:717
